TPU v7x, 512 devices: a whole 4x8x8 slice. The times are simulated.
512 devices in a mesh: dp: 8 (over x, y_hi), seq: 64 (over z, y_lo, core).
Axes of the slice: x: 4, y: 8 (y_hi: 2, y_lo: 4; y = y_hi * 4 + y_lo), z: 8, core: 2. Of those that a mesh axis runs over, the one named last changes fastest.
Arguments:
- points: bfloat16 [8, 16384, 384], P('dp', 'seq'), may hold values from -6 to 6
- cotangent: bfloat16 [8, 16384, 384], P('dp', 'seq'), may hold values from -6 to 6
- in_gain: float32 [384], replicated, may hold values from 0.5 to 2
- out_gain: float32 [384], replicated, may hold values from 0.5 to 2
- left_factor: bfloat16 [256, 256], replicated, may hold values from -0.375 to 0.375
- right_factor: bfloat16 [64, 64], replicated, may hold values from -0.75 to 0.75
- norm_gain: float32 [384], replicated, may hold values from 0.5 to 2
- gate_weight: bfloat16 [4, 96, 384], P(None, None, 'dp'), may hold values from -0.625 to 0.625
- up_weight: bfloat16 [4, 96, 384], P(None, None, 'dp'), may hold values from -0.625 to 0.625
- down_weight: bfloat16 [4, 96, 384], P(None, None, 'dp'), may hold values from -0.3125 to 0.3125
Outputs:
- layer_out: bfloat16 [8, 16384, 384], P('dp', 'seq')
- grad_points: bfloat16 [8, 16384, 384], P('dp', 'seq')
- grad_left: float32 [256, 256], replicated
- grad_right: float32 [64, 64], replicated
- grad_in_gain: float32 [384], replicated
- grad_out_gain: float32 [384], replicated
- grad_norm_gain: float32 [384], replicated
- grad_gate: float32 [4, 96, 384], P(None, None, 'dp')
- grad_up: float32 [4, 96, 384], P(None, None, 'dp')
- grad_down: float32 [4, 96, 384], P(None, None, 'dp')
All inputs are finite; a program needn't handle non-finite values.
Results may differ from a plain program's by a relative error of at most 0.0091.
Values may be sent and summed in bfloat16 or wider, within the bound.
A program may use at most 64 MiB of HBM per device.

v0:
```python
import jax
import jax.numpy as jnp
from jax import lax
from jax.sharding import PartitionSpec as P


def shards(
    points,
    cotangent,
    in_gain,
    out_gain,
    left_factor,
    right_factor,
    norm_gain,
    gate_weight,
    up_weight,
    down_weight,
):
    seq_count = lax.axis_size("seq")
    data_count = lax.axis_size("dp")
    row_count = points.shape[1]
    channels = points.shape[2]
    block_size = left_factor.shape[0]
    block_total = right_factor.shape[0]
    blocks = row_count // block_size
    shard_width = gate_weight.shape[2]
    gate_full, up_full, down_full = (
        lax.all_gather(gate_weight, "dp", axis=2, tiled=True),
        lax.all_gather(up_weight, "dp", axis=2, tiled=True),
        lax.all_gather(down_weight, "dp", axis=2, tiled=True),
    )
    nblocks = gate_full.shape[0]
    block_in = gate_full.shape[1]
    block_hidden = gate_full.shape[2]
    quarter = block_hidden // nblocks
    inputs = points[0].astype(jnp.float32)
    scaled = (inputs * in_gain).astype(jnp.bfloat16).reshape(blocks, block_size, channels)
    first_mix = jnp.einsum(
        "pb,abc->apc", left_factor, scaled, preferred_element_type=jnp.float32
    ).astype(jnp.bfloat16)
    received = lax.all_to_all(first_mix, "seq", split_axis=1, concat_axis=0, tiled=True)
    mixed = jnp.einsum("qa,apc->pqc", right_factor, received, preferred_element_type=jnp.float32)
    first_moved = received
    mixed = mixed.reshape(row_count, channels)
    residual = inputs + out_gain * mixed
    inv_rms = lax.rsqrt(jnp.mean(residual * residual, axis=-1, keepdims=True) + 1e-05)
    normed = residual * inv_rms
    hidden_in = (normed * norm_gain).astype(jnp.bfloat16).reshape(row_count, nblocks, block_in)
    gate_pre = jnp.einsum("rkd,kdf->rkf", hidden_in, gate_full, preferred_element_type=jnp.float32)
    up_pre = jnp.einsum("rkd,kdf->rkf", hidden_in, up_full, preferred_element_type=jnp.float32)
    sig_gate = jax.nn.sigmoid(gate_pre)
    act_gate = gate_pre * sig_gate
    hidden = (act_gate * up_pre).astype(jnp.bfloat16)
    hidden_grid = hidden.reshape(row_count, nblocks, nblocks, quarter)
    down_grid = down_full.reshape(nblocks, block_in, nblocks, quarter)
    branch = jnp.einsum(
        "rkjf,jokf->rjo", hidden_grid, down_grid, preferred_element_type=jnp.float32
    ).reshape(row_count, channels)
    layer_out = (residual + branch).astype(jnp.bfloat16)
    grad_grid = cotangent[0].reshape(row_count, nblocks, block_in)
    dhidden = jnp.einsum(
        "rjo,jokf->rkjf", grad_grid, down_grid, preferred_element_type=jnp.float32
    ).reshape(row_count, nblocks, block_hidden)
    grad_down = jnp.einsum(
        "rjo,rkjf->jokf", grad_grid, hidden_grid, preferred_element_type=jnp.float32
    ).reshape(nblocks, block_in, block_hidden)
    dgate = (dhidden * up_pre * sig_gate * (1.0 + gate_pre * (1.0 - sig_gate))).astype(jnp.bfloat16)
    dupper = (dhidden * act_gate).astype(jnp.bfloat16)
    dhid_in = jnp.einsum("rkf,kdf->rkd", dgate, gate_full, preferred_element_type=jnp.float32)
    dhid_in = (
        dhid_in + jnp.einsum("rkf,kdf->rkd", dupper, up_full, preferred_element_type=jnp.float32)
    ).reshape(row_count, channels)
    grad_gate = jnp.einsum("rkd,rkf->kdf", hidden_in, dgate, preferred_element_type=jnp.float32)
    grad_up = jnp.einsum("rkd,rkf->kdf", hidden_in, dupper, preferred_element_type=jnp.float32)
    grad_norm = jnp.sum(dhid_in * normed, axis=0)
    scaled_grad = dhid_in * norm_gain
    dresid = cotangent[0].astype(jnp.float32) + inv_rms * (
        scaled_grad - normed * jnp.mean(scaled_grad * normed, axis=-1, keepdims=True)
    )
    grad_out = jnp.sum(dresid * mixed, axis=0)
    dmixed = (
        (dresid * out_gain)
        .astype(jnp.bfloat16)
        .reshape(block_size // seq_count, block_total, channels)
    )
    dfirst = jnp.einsum(
        "qa,pqc->apc", right_factor, dmixed, preferred_element_type=jnp.float32
    ).astype(jnp.bfloat16)
    grad_right = jnp.einsum("pqc,apc->qa", dmixed, first_moved, preferred_element_type=jnp.float32)
    received = lax.all_to_all(dfirst, "seq", split_axis=0, concat_axis=1, tiled=True)
    dscaled = jnp.einsum("pb,apc->abc", left_factor, received, preferred_element_type=jnp.float32)
    grad_left = jnp.einsum("apc,abc->pb", received, scaled, preferred_element_type=jnp.float32)
    dscaled = dscaled.reshape(row_count, channels)
    grad_in = jnp.sum(dscaled * inputs, axis=0)
    grad_points = (dresid + dscaled * in_gain).astype(jnp.bfloat16)
    factor = float(data_count * row_count * seq_count) ** (-0.5)
    totals = lax.psum(
        (grad_gate, grad_up, grad_down, grad_left, grad_right, grad_in, grad_out, grad_norm),
        ("dp", "seq"),
    )
    start = lax.axis_index("dp") * shard_width
    gate_sum = lax.dynamic_slice_in_dim(totals[0], start, shard_width, 2)
    up_sum = lax.dynamic_slice_in_dim(totals[1], start, shard_width, 2)
    down_sum = lax.dynamic_slice_in_dim(totals[2], start, shard_width, 2)
    left_sum, right_sum, in_sum, out_sum, norm_sum = (
        totals[3],
        totals[4],
        totals[5],
        totals[6],
        totals[7],
    )
    return (
        layer_out[None],
        grad_points[None],
        left_sum * factor,
        right_sum * factor,
        in_sum * factor,
        out_sum * factor,
        norm_sum * factor,
        gate_sum * factor,
        up_sum * factor,
        down_sum * factor,
    )


def solution(mesh):
    in_specs = (
        P("dp", "seq", None),
        P("dp", "seq", None),
        P(),
        P(),
        P(),
        P(),
        P(),
        P(None, None, "dp"),
        P(None, None, "dp"),
        P(None, None, "dp"),
    )
    out_specs = (
        P("dp", "seq", None),
        P("dp", "seq", None),
        P(),
        P(),
        P(),
        P(),
        P(),
        P(None, None, "dp"),
        P(None, None, "dp"),
        P(None, None, "dp"),
    )
    return jax.shard_map(shards, mesh=mesh, in_specs=in_specs, out_specs=out_specs, check_vma=False)
```

profile of v0, /device:TPU:1, one launch (start us, length us, event | category | flops | bytes accessed | tf_op | source)
XLA Modules:
  0.0 498.9 jit_solution(1939229281374899762)
XLA Ops:
  7.2 0.9 copy-done
  8.1 1.2 fusion.8
  10.3 1.8 reduce.5
  12.1 0.8 reshape.326
  12.9 15.6 %all-to-all-start = ((bf16[64,2,768]{2,1,0:T(2,128)(2,1)}), bf16[64,2,768]{2,1,0:T(2,128)(2,1)}, u32[]{:S(2)}, u32[]{:S(2)}) async-start(bf16[64,2,768]{2,1,0:T(2,128)(2,1)} %reshape.326), calls=%async_computation | async-start | bytes 393216 | tf_op jit(solution)/shard_map/all_to_all | solution.py:41
  28.5 41.3 %all_gather.11 = bf16[4,96,384]{1,2,0:T(8,128)(2,1)S(1)} all-gather(bf16[4,96,48]{1,2,0:T(8,128)(2,1)S(1)} %copy-done.15), channel_id=1, replica_groups=mesh['dp'=8,'seq'=64] {'dp'}, dimensions={2}, use_global_device_ids=true | all-gather | bytes 331776 | tf_op jit(solution)/shard_map/all_gather | solution.py:30
  70.4 0.9 copy.60
  71.2 0.8 convert_element_type.81
  72.4 1.6 copy.69
  74.0 39.2 %all_gather.10 = bf16[4,96,384]{1,2,0:T(8,128)(2,1)S(1)} all-gather(bf16[4,96,48]{1,2,0:T(8,128)(2,1)S(1)} %copy-done.16), channel_id=1, replica_groups=mesh['dp'=8,'seq'=64] {'dp'}, dimensions={2}, use_global_device_ids=true | all-gather | bytes 331776 | tf_op jit(solution)/shard_map/all_gather | solution.py:29
  113.2 40.2 %all_gather.9 = bf16[4,96,384]{1,2,0:T(8,128)(2,1)S(1)} all-gather(bf16[4,96,48]{1,2,0:T(8,128)(2,1)S(1)} %copy-done.17), channel_id=1, replica_groups=mesh['dp'=8,'seq'=64] {'dp'}, dimensions={2}, use_global_device_ids=true | all-gather | bytes 331776 | tf_op jit(solution)/shard_map/all_gather | solution.py:28
  153.4 1.5 reshape.327
  155.0 1.1 bitcast_reduce_fusion
  157.8 0.8 copy-done.8
  158.6 2.0 multiply_convert_fusion
  160.9 1.3 fusion.32
  162.2 1.3 fusion.33
  164.1 0.9 copy.71
  165.7 0.9 copy.65
  167.2 1.2 multiply_reduce_fusion.1
  168.7 0.8 copy.74
  169.5 26.1 %all-to-all-start.1 = ((bf16[64,4,384]{2,1,0:T(4,128)(2,1)}), bf16[64,4,384]{2,1,0:T(4,128)(2,1)S(1)}, u32[]{:S(2)}, u32[]{:S(2)}) async-start(bf16[64,4,384]{2,1,0:T(4,128)(2,1)} %copy.74), calls=%async_computation.1 | async-start | bytes 393216 | tf_op jit(solution)/shard_map/all_to_all | solution.py:90
  196.0 1.2 fusion.10
  197.3 10.3 %all-to-all-done.1 = bf16[64,4,384]{2,1,0:T(4,128)(2,1)S(1)} async-done(((bf16[64,4,384]{2,1,0:T(4,128)(2,1)}), bf16[64,4,384]{2,1,0:T(4,128)(2,1)S(1)}, u32[]{:S(2)}, u32[]{:S(2)}) %all-to-all-start.1) | async-done | bytes 196640 | tf_op jit(solution)/shard_map/all_to_all | solution.py:90
  207.7 1.0 fusion.25
  208.8 1.0 fusion.18
  209.9 99.0 %all-reduce = (f32[64,64]{1,0:T(8,128)S(1)}, f32[384]{0:T(512)S(1)}, f32[384]{0:T(512)S(1)}, f32[384]{0:T(512)S(1)}) all-reduce(f32[64,64]{1,0:T(8,128)S(1)} %convolution_bitcast_fusion.1, f32[384]{0:T(512)S(1)} %fusion.12, f32[384]{0:T(512)S(1)} %get-tuple-element.20, ...), channel_id=1, replica_groups=mesh['dp'=8,'seq'=64] {'dp','seq'}, use_global_device_ids=true, to_apply=%region_3.0 | all-reduce | flops 5248 | bytes 41984 | tf_op jit(solution)/shard_map/psum | solution.py:97
  310.1 0.6 broadcast_multiply_fusion.1
  310.7 176.4 %all-reduce.4.cloned.1.call-done = (f32[256,256]{1,0:T(8,128)}, f32[4,96,384]{1,2,0:T(8,128)}, f32[4,96,384]{1,2,0:T(8,128)}, f32[4,96,384]{1,2,0:T(8,128)}) async-done(((f32[256,256]{1,0:T(8,128)}, f32[4,96,384]{1,2,0:T(8,128)}, f32[4,96,384]{1,2,0:T(8,128)}, f32[4,96,384]{1,2,0:T(8,128)}), (f32[256,256]{1,0:T(8,128)}, f32[4,96,384]{1,2,0:T(8,128)}, f32[4,96,384]{1,2,0:T(8,128)}, ...) | async-done | bytes 2031632 | tf_op jit(solution)/shard_map/psum | solution.py:97
  487.2 1.7 broadcast_multiply_fusion
  488.9 1.5 dynamic-slice_multiply_fusion.2
  490.4 1.6 dynamic-slice_multiply_fusion
  (72 shorter events, 7.5 us)
Async XLA Ops:
  7.2 0.9 copy-start
  7.2 21.3 %copy-start.15 = (bf16[4,96,48]{1,2,0:T(8,128)(2,1)S(1)}, bf16[4,96,48]{1,2,0:T(8,128)(2,1)}, u32[]{:S(2)}) copy-start(bf16[4,96,48]{1,2,0:T(8,128)(2,1)} %param.19) | copy-start | bytes 110596
  7.2 62.6 %copy-start.6 = (bf16[1,256,384]{2,1,0:T(8,128)(2,1)S(1)}, bf16[1,256,384]{2,1,0:T(8,128)(2,1)}, u32[]{:S(2)}) copy-start(bf16[1,256,384]{2,1,0:T(8,128)(2,1)} %param.11) | copy-start | bytes 589828
  12.9 140.5 %all-to-all-start = ((bf16[64,2,768]{2,1,0:T(2,128)(2,1)}), bf16[64,2,768]{2,1,0:T(2,128)(2,1)}, u32[]{:S(2)}, u32[]{:S(2)}) async-start(bf16[64,2,768]{2,1,0:T(2,128)(2,1)} %reshape.326), calls=%async_computation | async-start | bytes 393216 | tf_op jit(solution)/shard_map/all_to_all | solution.py:41
  28.5 41.9 %copy-start.1 = (bf16[1,256,384]{2,1,0:T(8,128)(2,1)S(1)}, bf16[1,256,384]{2,1,0:T(8,128)(2,1)}, u32[]{:S(2)}) copy-start(bf16[1,256,384]{2,1,0:T(8,128)(2,1)} %param.10) | copy-start | bytes 589828
  69.8 1.4 copy-start.2
  70.0 2.1 copy-start.4
  70.0 2.1 copy-start.19
  70.0 2.1 copy-start.13
  72.3 1.7 copy-start.16
  72.4 40.8 %copy-start.17 = (bf16[4,96,48]{1,2,0:T(8,128)(2,1)S(1)}, bf16[4,96,48]{1,2,0:T(8,128)(2,1)}, u32[]{:S(2)}) copy-start(bf16[4,96,48]{1,2,0:T(8,128)(2,1)} %param.17) | copy-start | bytes 110596
  74.0 82.2 %copy-start.14 = (bf16[64,64]{1,0:T(8,128)(2,1)S(1)}, bf16[64,64]{1,0:T(8,128)(2,1)}, u32[]{:S(2)}) copy-start(bf16[64,64]{1,0:T(8,128)(2,1)} %param.15) | copy-start | bytes 24580
  156.2 1.0 copy-start.9
  157.2 1.4 copy-start.8
  163.6 1.5 copy-start.12
  164.1 1.2 copy-start.3
  165.7 1.5 copy-start.7
  167.2 28.8 %copy-start.5 = (bf16[1,256,384]{1,2,0:T(8,128)(2,1)S(1)}, bf16[1,256,384]{1,2,0:T(8,128)(2,1)}, u32[]{:S(2)}) copy-start(bf16[1,256,384]{1,2,0:T(8,128)(2,1)} %copy-done.4) | copy-start | bytes 589828
  169.5 38.1 %copy-start.18 = (f32[384]{0:T(512)S(1)}, f32[384]{0:T(512)}, u32[]{:S(2)}) copy-start(f32[384]{0:T(512)} %param.12) | copy-start | bytes 4612
  169.5 38.1 %all-to-all-start.1 = ((bf16[64,4,384]{2,1,0:T(4,128)(2,1)}), bf16[64,4,384]{2,1,0:T(4,128)(2,1)S(1)}, u32[]{:S(2)}, u32[]{:S(2)}) async-start(bf16[64,4,384]{2,1,0:T(4,128)(2,1)} %copy.74), calls=%async_computation.1 | async-start | bytes 393216 | tf_op jit(solution)/shard_map/all_to_all | solution.py:90
  195.7 291.5 %all-reduce.4.cloned.1.call-start = ((), (), s32[]{:S(2)}) async-start(), calls=%async_computation.2 | async-start | bytes 5242880 | tf_op jit(solution)/shard_map/psum | solution.py:97
  207.7 1.0 copy-start.10
  207.7 1.1 copy-start.11
Sparse Core Ops, SparseCore 0:
  208.8 278.3 all-reduce.3
where the time goes:
time: 501 us; the launch traced here: 499 us
  blocking collectives  220 us (44%)
  waiting for transfers between devices  187 us (37%)
  starting transfers between devices  41.8 us (8%)
  between operations  14.4 us (3%)
  local copies, waits for them, and re-layouts  13.6 us (3%)
  matrix products  11.6 us (2%)
  other arithmetic  10.9 us (2%)
    psum x1, waiting for transfers between devices, shards(): lax.psum((grad_gate, grad_up, grad_down, grad_left, grad_right, grad_in,...  176 us
    psum x1, blocking collectives, shards(): lax.psum((grad_gate, grad_up, grad_down, grad_left, grad_right, grad_in,...  99 us
    all_gather x1, blocking collectives, shards(): lax.all_gather(down_weight, 'dp', axis=2, tiled=True)  41.3 us
    all_gather x1, blocking collectives, shards(): lax.all_gather(gate_weight, 'dp', axis=2, tiled=True)  40.2 us
    all_gather x1, blocking collectives, shards(): lax.all_gather(up_weight, 'dp', axis=2, tiled=True)  39.2 us
    all_to_all x1, starting transfers between devices, shards(): lax.all_to_all(dfirst, 'seq', split_axis=0, concat_axis=1, tiled=True)  26.1 us
    all_to_all x1, starting transfers between devices, shards(): lax.all_to_all(first_mix, 'seq', split_axis=1, concat_axis=0, tiled=True)  15.6 us
    all_to_all x1, waiting for transfers between devices, shards(): lax.all_to_all(dfirst, 'seq', split_axis=0, concat_axis=1, tiled=True)  10.3 us
  transfers between devices with their start and end apart: 3, of which 2 were waited for; matrix products, arithmetic and copies ran while one was open for 2% of the time, Pallas kernels for 0%

commit v1 on v0

v1 whole, which is shorter than its diff:
```python
import functools

import jax
import jax.numpy as jnp
from jax import lax
from jax.experimental import pallas as pl
from jax.experimental.pallas import tpu as pltpu
from jax.sharding import PartitionSpec as P

MESH = pl.DeviceIdType.MESH
SLOT = 96
REP = 80


def place():
    d = lax.axis_index("dp")
    s = lax.axis_index("seq")
    return d // 2, d % 2, s // 8, (s // 2) % 4, s % 2


def device(x, yh, z, yl, c):
    return (x * 2 + yh, (z * 4 + yl) * 2 + c)


def greet(peers):
    barrier = pltpu.get_barrier_semaphore()
    for peer in peers:
        pl.semaphore_signal(barrier, inc=1, device_id=peer, device_id_type=MESH)
    pl.semaphore_wait(barrier, len(peers))


def gather_kernel(w_ref, out_ref, local_sem, send_sem, recv_sem):
    x, yh, z, yl, c = place()
    pair = device(x, yh, z, yl, 1 - c)
    xs = [device((x + k) % 4, yh, z, yl, c) for k in (1, 2, 3)]
    across = [device(x, 1 - yh, z, k, c) for k in range(4)]
    width = w_ref.shape[1]
    half = w_ref.shape[0] // 2

    def part(d):
        at = pl.ds(pl.multiple_of(d * width, 16), width)
        return out_ref.at[pl.ds(half * c, half), at, :]

    def remote(src, dst, sent, got, peer):
        return pltpu.make_async_remote_copy(
            src, dst, send_sem.at[sent], recv_sem.at[got], device_id=peer, device_id_type=MESH
        )

    greet([pair] + xs + across)
    own = w_ref.at[pl.ds(half * c, half)]
    mine = part(x * 2 + yh)
    theirs = part(x * 2 + 1 - yh)
    end = (yl == 0) | (yl == 3)
    base = 2 - 2 * (yl // 3)
    over = [
        remote(own, mine, n, 0, device(x, 1 - yh, z, base + n, c)) for n in range(2)
    ]

    @pl.when(end)
    def _():
        for copy in over:
            copy.start()

    local = pltpu.make_async_copy(own, mine, local_sem)
    local.start()
    sends = [remote(own, mine, 2 + n, 1 + n, peer) for n, peer in enumerate(xs)]
    for copy in sends:
        copy.start()
    over[0].wait_recv()
    for n, peer in enumerate(xs):
        copy = remote(theirs, theirs, 5 + n, 4 + n, peer)
        copy.start()
        sends.append(copy)
    local.wait()
    for copy in sends:
        copy.wait_recv()
    whole = out_ref.at[pl.ds(half * c, half)]
    copy = remote(whole, whole, 8, 7, pair)
    copy.start()
    copy.wait_recv()
    for copy in sends + [copy]:
        copy.wait_send()

    @pl.when(end)
    def _():
        for copy in over:
            copy.wait_send()


def gather_weights(w):
    n, width, d = w.shape
    return pl.pallas_call(
        gather_kernel,
        out_shape=jax.ShapeDtypeStruct((n, 8 * width, d), w.dtype),
        in_specs=[pl.BlockSpec(memory_space=pltpu.VMEM)],
        out_specs=pl.BlockSpec(memory_space=pltpu.VMEM),
        scratch_shapes=[
            pltpu.SemaphoreType.DMA,
            pltpu.SemaphoreType.DMA((9,)),
            pltpu.SemaphoreType.DMA((8,)),
        ],
        compiler_params=pltpu.CompilerParams(collective_id=1, has_side_effects=True),
        cost_estimate=pl.CostEstimate(flops=0, bytes_accessed=40_000_000, transcendentals=0),
        name="gather_weights",
    )(w)


PIECES = (
    ((0, 0, 0, 48),),
    ((0, 48, 0, 32), (1, 0, 32, 16)),
    ((1, 16, 0, 48),),
    ((2, 0, 0, 48),),
    ((2, 48, 0, 32), (3, 0, 32, 16)),
    ((3, 16, 0, 48),),
)


def sum_kernel(
    factor,
    gate_ref, up_ref, down_ref, left_ref, right_ref, in_ref, outg_ref, norm_ref,
    out_ref,
    rep_ref, wgot, rgot, xsend, xgot, ysend, ygot, zall, yall, wother, repall,
    send_sem, recv_sem,
):
    x, yh, z, yl, c = place()
    f32, bf16 = jnp.float32, jnp.bfloat16
    y = yh * 4 + yl
    pair = device(x, yh, z, yl, 1 - c)
    xs = [device((x + k) % 4, yh, z, yl, c) for k in (1, 2, 3)]
    xo = [device((x + k) % 4, yh, z, yl, 1 - c) for k in (1, 2, 3)]
    near = [device(x, yh, z, (yl + k) % 4, c) for k in (1, 2, 3)]
    far = [device(x, 1 - yh, z, (yl + k) % 4, c) for k in (0, 1, 2, 3)]
    zs = [device(x, yh, (z + k) % 8, yl, c) for k in range(1, 8)]
    greet([pair] + xs + xo + near + far + zs)
    started = []

    def send(src, dst, peer):
        n = len(started)
        copy = pltpu.make_async_remote_copy(
            src, dst, send_sem.at[n], recv_sem.at[n], device_id=peer, device_id_type=MESH
        )
        copy.start()
        started.append(copy)
        return copy

    def landed(copies):
        for copy in copies:
            copy.wait_recv()

    grads = (gate_ref, up_ref, down_ref)
    copies = [
        send(ref.at[pl.ds(2 * (1 - c), 2)], wgot.at[kind], pair)
        for kind, ref in enumerate(grads)
    ]
    for k in range(4):
        for n in range(8):
            row, lane = (k % 2) * 128 + n * 16, (k // 2) * 128
            rep_ref[0, k, n] = left_ref[row : row + 16, lane : lane + 128].astype(bf16)
            rep_ref[1, k, n] = jnp.zeros((16, 128), bf16)
    for n in range(2):
        for j in range(2):
            at = slice(32 * j + 16 * n, 32 * j + 16 * n + 16)
            rep_ref[1, 0, n, :, 64 * j : 64 * j + 64] = right_ref[at, :].astype(bf16)
    gains = [
        ref[128 * t : 128 * t + 128].reshape(1, 128)
        for ref in (in_ref, outg_ref, norm_ref)
        for t in range(3)
    ]
    gains.append(jnp.zeros((7, 128), f32))
    rep_ref[1, 0, 2] = jnp.concatenate(gains, axis=0).astype(bf16)
    copies.append(send(rep_ref.at[1 - c], rgot, pair))
    for dest in range(4):
        for h in range(2):
            for q in range(4):
                xsend[dest, h * 4 + q, 0:REP, 96:128] = jnp.zeros((REP, 32), bf16)
            for q in (1, 3):
                xsend[dest, h * 4 + q, 64:REP] = jnp.zeros((REP - 64, 128), bf16)
    landed(copies)
    for dest in range(4):
        for h in range(2):
            first = (dest * 2 + h) * 48
            for i, pieces in enumerate(PIECES):
                kind, k = divmod(i, 2)
                for q, row, start, rows in pieces:
                    at = slice(first + start, first + start + rows)
                    total = grads[kind][2 * c + k, at, :].astype(f32)
                    total = total + wgot[kind, k, at, :].astype(f32)
                    xsend[dest, h * 4 + q, row : row + rows, 0:96] = total.astype(bf16)
        total = rep_ref[c, dest].astype(f32) + rgot[dest].astype(f32)
        xsend[dest, :, REP:SLOT, :] = total.astype(bf16)

    copies = [
        send(xsend.at[(x + k) % 4], xgot.at[k - 1], peer) for k, peer in zip((1, 2, 3), xs)
    ]
    landed(copies)

    def add_x(n, carry):
        total = xsend[x, n].astype(f32)
        for k in range(3):
            total = total + xgot[k, n].astype(f32)
        ysend[n] = total.astype(bf16)
        return carry

    lax.fori_loop(0, 8, add_x, 0)

    copies = [
        send(ysend.at[yh * 4 + (yl + k) % 4], ygot.at[k - 1], peer)
        for k, peer in zip((1, 2, 3), near)
    ]
    copies += [
        send(ysend.at[(1 - yh) * 4 + (yl + k) % 4], ygot.at[3 + k], peer)
        for k, peer in zip((0, 1, 2, 3), far)
    ]
    landed(copies)
    total = ysend[y].astype(f32)
    for k in range(7):
        total = total + ygot[k].astype(f32)
    zall[z] = total.astype(bf16)

    landed([send(zall.at[z], zall.at[z], peer) for peer in zs])
    total = zall[0].astype(f32)
    for k in range(1, 8):
        total = total + zall[k].astype(f32)
    yall[y] = total.astype(bf16)

    copies = [send(yall.at[y], yall.at[y], peer) for peer in near]
    tail = yall.at[y, REP:SLOT]
    copies += [send(tail, tail, peer) for peer in far]
    landed(copies)
    copies = [send(yall.at[pl.ds(4 * yh, 4)], wother, pair)]
    tails = yall.at[:, REP:SLOT]
    copies += [send(tails, repall.at[c, x], peer) for peer in [pair] + xs + xo]
    repall[c, x] = yall[:, REP:SLOT, :]

    def unpack(chunk, core):
        for i, pieces in enumerate(PIECES):
            kind, k = divmod(i, 2)
            for q, row, start, rows in pieces:
                at = pl.multiple_of(kind * 192 + (2 * core + k) * 48 + start, 16)
                value = chunk(q)[row : row + rows, 0:96].astype(f32) * factor
                out_ref[pl.ds(at, rows), 256:352] = value

    unpack(lambda q: yall.at[4 * yh + q], c)
    landed(copies)
    unpack(lambda q: wother.at[q], 1 - c)
    for k in range(4):
        for n in range(8):
            row, lane = (k % 2) * 128 + n * 16, (k // 2) * 128
            value = repall[0, k, n].astype(f32) * factor
            out_ref[row : row + 16, lane : lane + 128] = value
    for n in range(2):
        value = repall[1, 0, n].astype(f32) * factor
        out_ref[256 + n * 16 : 272 + n * 16, 0:64] = value[:, 0:64]
        out_ref[288 + n * 16 : 304 + n * 16, 0:64] = value[:, 64:128]
    value = repall[1, 0, 2].astype(f32) * factor
    for j in range(3):
        for t in range(3):
            row = value[3 * j + t : 3 * j + t + 1, :]
            out_ref[576 + j : 577 + j, t * 128 : t * 128 + 128] = row
    for copy in started:
        copy.wait_send()


def sum_gradients(grads, factor):
    vmem = pl.BlockSpec(memory_space=pltpu.VMEM)
    bf16 = jnp.bfloat16
    copies = 4 + 3 + 7 + 7 + 7 + 8
    return pl.pallas_call(
        functools.partial(sum_kernel, factor),
        out_shape=jax.ShapeDtypeStruct((584, 384), jnp.float32),
        in_specs=[vmem] * len(grads),
        out_specs=vmem,
        scratch_shapes=[
            pltpu.VMEM((2, 4, 8, 16, 128), bf16),
            pltpu.VMEM((3, 2, 384, 96), bf16),
            pltpu.VMEM((4, 8, 16, 128), bf16),
            pltpu.VMEM((4, 8, SLOT, 128), bf16),
            pltpu.VMEM((3, 8, SLOT, 128), bf16),
            pltpu.VMEM((8, SLOT, 128), bf16),
            pltpu.VMEM((7, SLOT, 128), bf16),
            pltpu.VMEM((8, SLOT, 128), bf16),
            pltpu.VMEM((8, SLOT, 128), bf16),
            pltpu.VMEM((4, SLOT, 128), bf16),
            pltpu.VMEM((2, 4, 8, 16, 128), bf16),
            pltpu.SemaphoreType.DMA((copies,)),
            pltpu.SemaphoreType.DMA((copies,)),
        ],
        compiler_params=pltpu.CompilerParams(collective_id=2, has_side_effects=True),
        name="sum_gradients",
    )(*grads)


def shards(
    points,
    cotangent,
    in_gain,
    out_gain,
    left_factor,
    right_factor,
    norm_gain,
    gate_weight,
    up_weight,
    down_weight,
):
    seq_count = lax.axis_size("seq")
    data_count = lax.axis_size("dp")
    row_count = points.shape[1]
    channels = points.shape[2]
    block_size = left_factor.shape[0]
    block_total = right_factor.shape[0]
    blocks = row_count // block_size
    shard_width = gate_weight.shape[2]
    nblocks, block_in = gate_weight.shape[:2]
    block_hidden = data_count * shard_width
    quarter = block_hidden // nblocks
    packed = jnp.concatenate([gate_weight, up_weight, down_weight], axis=0).transpose(0, 2, 1)
    weights = gather_weights(packed)
    gate_full, up_full, down_full = weights[0:4], weights[4:8], weights[8:12]
    inputs = points[0].astype(jnp.float32)
    scaled = (inputs * in_gain).astype(jnp.bfloat16).reshape(blocks, block_size, channels)
    first_mix = jnp.einsum(
        "pb,abc->apc", left_factor, scaled, preferred_element_type=jnp.float32
    ).astype(jnp.bfloat16)
    received = lax.all_to_all(first_mix, "seq", split_axis=1, concat_axis=0, tiled=True)
    mixed = jnp.einsum("qa,apc->pqc", right_factor, received, preferred_element_type=jnp.float32)
    first_moved = received
    mixed = mixed.reshape(row_count, channels)
    residual = inputs + out_gain * mixed
    inv_rms = lax.rsqrt(jnp.mean(residual * residual, axis=-1, keepdims=True) + 1e-05)
    normed = residual * inv_rms
    hidden_in = (normed * norm_gain).astype(jnp.bfloat16).reshape(row_count, nblocks, block_in)
    gate_pre = jnp.einsum("rkd,kfd->rkf", hidden_in, gate_full, preferred_element_type=jnp.float32)
    up_pre = jnp.einsum("rkd,kfd->rkf", hidden_in, up_full, preferred_element_type=jnp.float32)
    sig_gate = jax.nn.sigmoid(gate_pre)
    act_gate = gate_pre * sig_gate
    hidden = (act_gate * up_pre).astype(jnp.bfloat16)
    hidden_grid = hidden.reshape(row_count, nblocks, nblocks, quarter)
    down_grid = down_full.reshape(nblocks, nblocks, quarter, block_in)
    branch = jnp.einsum(
        "rkjf,jkfo->rjo", hidden_grid, down_grid, preferred_element_type=jnp.float32
    ).reshape(row_count, channels)
    layer_out = (residual + branch).astype(jnp.bfloat16)
    grad_grid = cotangent[0].reshape(row_count, nblocks, block_in)
    dhidden = jnp.einsum(
        "rjo,jkfo->rkjf", grad_grid, down_grid, preferred_element_type=jnp.float32
    ).reshape(row_count, nblocks, block_hidden)
    grad_down = jnp.einsum(
        "rjo,rkjf->jkfo", grad_grid, hidden_grid, preferred_element_type=jnp.float32
    ).reshape(nblocks, block_hidden, block_in)
    dgate = (dhidden * up_pre * sig_gate * (1.0 + gate_pre * (1.0 - sig_gate))).astype(jnp.bfloat16)
    dupper = (dhidden * act_gate).astype(jnp.bfloat16)
    dhid_in = jnp.einsum("rkf,kfd->rkd", dgate, gate_full, preferred_element_type=jnp.float32)
    dhid_in = (
        dhid_in + jnp.einsum("rkf,kfd->rkd", dupper, up_full, preferred_element_type=jnp.float32)
    ).reshape(row_count, channels)
    grad_gate = jnp.einsum("rkd,rkf->kfd", hidden_in, dgate, preferred_element_type=jnp.float32)
    grad_up = jnp.einsum("rkd,rkf->kfd", hidden_in, dupper, preferred_element_type=jnp.float32)
    grad_norm = jnp.sum(dhid_in * normed, axis=0)
    scaled_grad = dhid_in * norm_gain
    dresid = cotangent[0].astype(jnp.float32) + inv_rms * (
        scaled_grad - normed * jnp.mean(scaled_grad * normed, axis=-1, keepdims=True)
    )
    grad_out = jnp.sum(dresid * mixed, axis=0)
    dmixed = (
        (dresid * out_gain)
        .astype(jnp.bfloat16)
        .reshape(block_size // seq_count, block_total, channels)
    )
    dfirst = jnp.einsum(
        "qa,pqc->apc", right_factor, dmixed, preferred_element_type=jnp.float32
    ).astype(jnp.bfloat16)
    grad_right = jnp.einsum("pqc,apc->qa", dmixed, first_moved, preferred_element_type=jnp.float32)
    received = lax.all_to_all(dfirst, "seq", split_axis=0, concat_axis=1, tiled=True)
    dscaled = jnp.einsum("pb,apc->abc", left_factor, received, preferred_element_type=jnp.float32)
    grad_left = jnp.einsum("apc,abc->pb", received, scaled, preferred_element_type=jnp.float32)
    dscaled = dscaled.reshape(row_count, channels)
    grad_in = jnp.sum(dscaled * inputs, axis=0)
    grad_points = (dresid + dscaled * in_gain).astype(jnp.bfloat16)
    factor = float(data_count * row_count * seq_count) ** (-0.5)
    sums = sum_gradients(
        (
            grad_gate.astype(jnp.bfloat16),
            grad_up.astype(jnp.bfloat16),
            grad_down.astype(jnp.bfloat16),
            grad_left,
            grad_right,
            grad_in,
            grad_out,
            grad_norm,
        ),
        factor,
    )

    def weight(n):
        part = sums[192 * n : 192 * n + 192, 256:352]
        return part.reshape(nblocks, shard_width, block_in).transpose(0, 2, 1)

    return (
        layer_out[None],
        grad_points[None],
        sums[0:256, 0:256],
        sums[256:320, 0:64],
        sums[576],
        sums[577],
        sums[578],
        weight(0),
        weight(1),
        weight(2),
    )


def solution(mesh):
    in_specs = (
        P("dp", "seq", None),
        P("dp", "seq", None),
        P(),
        P(),
        P(),
        P(),
        P(),
        P(None, None, "dp"),
        P(None, None, "dp"),
        P(None, None, "dp"),
    )
    out_specs = (
        P("dp", "seq", None),
        P("dp", "seq", None),
        P(),
        P(),
        P(),
        P(),
        P(),
        P(None, None, "dp"),
        P(None, None, "dp"),
        P(None, None, "dp"),
    )
    return jax.shard_map(shards, mesh=mesh, in_specs=in_specs, out_specs=out_specs, check_vma=False)
```

time: 501 us -> 139 us (0.28)
  blocking collectives: 220 us -> 0 us
  waiting for transfers between devices: 187 us -> 6.29 us
  Pallas kernels: 0 us -> 65.4 us
  starting transfers between devices: 41.8 us -> 24.6 us
  between operations: 14.4 us -> 1 us
  local copies, waits for them, and re-layouts: 13.6 us -> 21.2 us
    psum x1 -> x0, waiting for transfers between devices: 176 us -> none  [shards(): lax.psum((grad_gate, grad_up, grad_down, grad_left, grad_right, grad_in,...]
    all_gather x3 -> x0, blocking collectives: 121 us -> none  [the longest x1 41.3 us: shards(): lax.all_gather(down_weight, 'dp', axis=2, tiled=True)]
    psum x1 -> x0, blocking collectives: 99 us -> none  [shards(): lax.psum((grad_gate, grad_up, grad_down, grad_left, grad_right, grad_in,...]
    pallas_call x0 -> x2, Pallas kernels: none -> 65.4 us  [the longest x1 45.5 us: sum_gradients(): pl.pallas_call(functools.partial(sum_kernel, factor), out_shape=jax.Shape...]
    all_to_all x1, starting transfers between devices: 26.1 us -> 9.16 us  [shards(): lax.all_to_all(dfirst, 'seq', split_axis=0, concat_axis=1, tiled=True)]
    slice x0 -> x5, local copies, waits for them, and re-layouts: none -> 7.19 us  [the longest x1 1.7 us: weight(): part = sums[192 * n:192 * n + 192, 256:352]]
    mul x6 -> x0, other arithmetic: 6.63 us -> none  [the longest x1 1.68 us: shards(): left_sum * factor]
  transfers between devices with their start and end apart: 3 -> 2, of which waited for: 2 -> 1; matrix products, arithmetic and copies ran while one was open for 2% -> 8% of each run, Pallas kernels for 0% -> 14%
where the time goes in v1:
time: 139 us; the launch traced here: 138 us
  Pallas kernels  65.4 us (47%)
  starting transfers between devices  24.6 us (18%)
  local copies, waits for them, and re-layouts  21.2 us (15%)
  matrix products  13.7 us (10%)
  waiting for transfers between devices  6.29 us (5%)
  other arithmetic  6.15 us (4%)
    pallas_call x1, Pallas kernels, sum_gradients(): pl.pallas_call(functools.partial(sum_kernel, factor), out_shape=jax.Shape...  45.5 us
    pallas_call x1, Pallas kernels, gather_weights(): pl.pallas_call(gather_kernel, out_shape=jax.ShapeDtypeStruct((n, 8 * widt...  20 us
    all_to_all x1, starting transfers between devices, shards(): lax.all_to_all(first_mix, 'seq', split_axis=1, concat_axis=0, tiled=True)  15.4 us
    all_to_all x1, starting transfers between devices, shards(): lax.all_to_all(dfirst, 'seq', split_axis=0, concat_axis=1, tiled=True)  9.16 us
    all_to_all x1, waiting for transfers between devices, shards(): lax.all_to_all(dfirst, 'seq', split_axis=0, concat_axis=1, tiled=True)  6.29 us
    unnamed x40, local copies, waits for them, and re-layouts  3.61 us
  transfers between devices with their start and end apart: 2, of which 1 were waited for; matrix products, arithmetic and copies ran while one was open for 8% of the time, Pallas kernels for 14%

profile of v1, /device:TPU:1, one launch (start us, length us, event | category | flops | bytes accessed | tf_op | source)
XLA Modules:
  0.0 138.3 jit_solution(13596254301723476384)
XLA Ops:
  0.7 0.9 copy-done
  1.6 1.2 fusion.9
  3.8 1.8 %reduce.11 = bf16[256,384]{1,0:T(8,128)(2,1)S(1)} reduce(bf16[256,1,384]{2,1,0:T(2,128)(2,1)S(1)} %bitcast.161, bf16[]{:T(256)} %broadcast.174), dimensions={1}, to_apply=%bitcast.129.reduce_sub_computation | reduce | bytes 393218
  5.6 0.8 reshape.339
  6.4 15.4 %all-to-all-start = ((bf16[64,2,768]{2,1,0:T(2,128)(2,1)}), bf16[64,2,768]{2,1,0:T(2,128)(2,1)S(1)}, u32[]{:S(2)}, u32[]{:S(2)}) async-start(bf16[64,2,768]{2,1,0:T(2,128)(2,1)} %reshape.339), calls=%async_computation | async-start | bytes 393216 | tf_op jit(solution)/shard_map/all_to_all | solution.py:324
  21.8 0.9 copy.96
  24.4 20.0 %gather_weights.1 = bf16[12,384,96]{2,1,0:T(8,128)(2,1)} custom-call(bf16[12,48,96]{2,1,0:T(8,128)(2,1)} %maximum_bitcast_fusion.w_ref), custom_call_target="tpu_custom_call" | custom-call | bytes 40000000 | tf_op jit(solution)/shard_map/gather_weights/pallas_call | solution.py:92
  44.4 1.0 slice.33
  45.9 1.3 copy.104
  47.4 1.1 bitcast_reduce_fusion
  49.2 1.0 copy.97
  50.3 1.3 multiply_convert_fusion.1
  51.9 1.0 copy-done.4
  53.0 1.9 %fusion.3 = (bf16[256,4,384]{0,2,1:T(8,128)(2,1)S(1)}, bf16[256,4,384]{0,2,1:T(8,128)(2,1)S(1)}, bf16[256,4,384]{0,2,1:T(8,128)(2,1)}) fusion(f32[256,4,4,96]{0,3,2,1:T(8,128)S(1)} %copy-done.4, f32[4,384,256]{2,1,0:T(8,128)S(1)} %fusion.31, bf16[12,384,96]{2,1,0:T(8,128)(2,1)S(1)} %copy-done.1, bf16[256,4,96]{0,2,1:T(8,128)(2,1)S(1)} %get-tuple-element.17), kind=kOutput, calls=%fused_computation.5 | convolution fusion | flops 81395712 | bytes 6586368 | tf_op jit(solution)/shard_map/rkd,kfd->rkf/dot_general | solution.py:332
  55.2 1.1 convolution_convert_fusion.2
  56.3 1.1 convolution_convert_fusion.1
  58.0 1.5 %fusion.12 = f32[4,96,256,1]{2,1,3,0:T(8,128)S(1)} fusion(bf16[4,4,96,96]{3,2,1,0:T(8,128)(2,1)S(1)} %bitcast.157, bf16[256,4,4,96]{0,3,2,1:T(8,128)(2,1)} %bitcast.165), kind=kOutput, calls=%fused_computation.26 | convolution fusion | flops 75497472 | bytes 1474560 | tf_op jit(solution)/shard_map/rkjf,jkfo->rjo/dot_general | solution.py:339
  59.5 0.9 copy.102
  62.0 0.8 copy.112
  62.9 9.2 %all-to-all-start.1 = ((bf16[64,4,384]{2,1,0:T(4,128)(2,1)}), bf16[64,4,384]{2,1,0:T(4,128)(2,1)S(1)}, u32[]{:S(2)}, u32[]{:S(2)}) async-start(bf16[64,4,384]{2,1,0:T(4,128)(2,1)} %copy.112), calls=%async_computation.1 | async-start | bytes 393216 | tf_op jit(solution)/shard_map/all_to_all | solution.py:373
  72.0 1.0 copy.117.gate_ref
  73.0 0.9 copy.118.up_ref
  74.6 0.8 convolution_bitcast_fusion.1.right_ref
  75.4 2.3 %convolution_convert_fusion = bf16[4,4,96,96]{3,2,1,0:T(8,128)(2,1)} fusion(bf16[256,4,96,1]{0,2,3,1:T(8,128)(2,1)S(1)} %bitcast.164, bf16[256,4,4,96]{0,3,2,1:T(8,128)(2,1)} %bitcast.166), kind=kOutput, calls=%fused_computation.16 | convolution fusion | flops 75644928 | bytes 1277952 | tf_op jit(solution)/shard_map/rjo,rkjf->jkfo/dot_general | solution.py:347
  77.7 6.3 %all-to-all-done.1 = bf16[64,4,384]{2,1,0:T(4,128)(2,1)S(1)} async-done(((bf16[64,4,384]{2,1,0:T(4,128)(2,1)}), bf16[64,4,384]{2,1,0:T(4,128)(2,1)S(1)}, u32[]{:S(2)}, u32[]{:S(2)}) %all-to-all-start.1) | async-done | bytes 196640 | tf_op jit(solution)/shard_map/all_to_all | solution.py:373
  84.0 1.0 fusion.25.left_ref
  85.0 1.0 fusion.20
  86.7 45.5 %sum_gradients.1 = f32[584,384]{1,0:T(8,128)} custom-call(bf16[4,384,96]{2,1,0:T(8,128)(2,1)} %copy.117.gate_ref, bf16[4,384,96]{2,1,0:T(8,128)(2,1)} %copy.118.up_ref, bf16[4,384,96]{2,1,0:T(8,128)(2,1)} %bitcast.167, f32[256,256]{1,0:T(8,128)} %fusion.25.left_ref, f32[64,64]{1,0:T(8,128)} %convolution_bitcast_fusion.1.right_ref, f32[384]{0:T(512)} %fusion.14.in_ref, ...), custom_call_target="tpu_custom_call" | custom-call | tf_op jit(solution)/shard_map/sum_gradients/pallas_call | solution.py:268
  132.1 1.7 %slice.36 = f32[256,256]{1,0:T(8,128)} slice(f32[584,384]{1,0:T(8,128)} %sum_gradients.1), slice={[0:256], [0:256]} | slice | bytes 524288 | tf_op jit(solution)/shard_map/slice | solution.py:401
  133.8 1.4 slice.37
  135.2 1.4 %slice_reduce_fusion = (f32[384]{0:T(512)}, f32[384]{0:T(512)}, f32[384]{0:T(512)}) fusion(f32[584,384]{1,0:T(8,128)} %sum_gradients.1), kind=kLoop, calls=%fused_computation.56 | loop fusion | bytes 9216 | tf_op jit(solution)/shard_map/slice | solution.py:405
  136.6 1.7 %fusion.30 = (f32[192,96]{1,0:T(8,128)}, f32[192,96]{1,0:T(8,128)}, f32[192,96]{1,0:T(8,128)}) fusion(f32[584,384]{1,0:T(8,128)} %sum_gradients.1), kind=kLoop, calls=%fused_computation.61 | loop fusion | bytes 442368 | tf_op jit(solution)/shard_map/slice | solution.py:395
  (63 shorter events, 8.4 us)
Async XLA Ops:
  0.6 0.9 copy-start
  0.7 21.2 %copy-start.2 = (bf16[1,256,384]{2,1,0:T(8,128)(2,1)S(1)}, bf16[1,256,384]{2,1,0:T(8,128)(2,1)}, u32[]{:S(2)}) copy-start(bf16[1,256,384]{2,1,0:T(8,128)(2,1)} %param.10) | copy-start | bytes 589828
  2.7 20.7 %copy-start.17 = (f32[384]{0:T(512)S(1)}, f32[384]{0:T(512)}, u32[]{:S(2)}) copy-start(f32[384]{0:T(512)} %param.16) | copy-start | bytes 4612
  2.8 20.8 %copy-start.11 = (f32[384]{0:T(512)S(1)}, f32[384]{0:T(512)}, u32[]{:S(2)}) copy-start(f32[384]{0:T(512)} %param.13) | copy-start | bytes 4612
  2.8 20.9 %copy-start.13 = (bf16[4,96,48]{1,2,0:T(8,128)(2,1)S(1)}, bf16[4,96,48]{1,2,0:T(8,128)(2,1)}, u32[]{:S(2)}) copy-start(bf16[4,96,48]{1,2,0:T(8,128)(2,1)} %param.19) | copy-start | bytes 110596
  2.8 20.9 %copy-start.14 = (bf16[4,96,48]{1,2,0:T(8,128)(2,1)S(1)}, bf16[4,96,48]{1,2,0:T(8,128)(2,1)}, u32[]{:S(2)}) copy-start(bf16[4,96,48]{1,2,0:T(8,128)(2,1)} %param.18) | copy-start | bytes 110596
  2.8 20.9 %copy-start.15 = (bf16[4,96,48]{1,2,0:T(8,128)(2,1)S(1)}, bf16[4,96,48]{1,2,0:T(8,128)(2,1)}, u32[]{:S(2)}) copy-start(bf16[4,96,48]{1,2,0:T(8,128)(2,1)} %param.17) | copy-start | bytes 110596
  6.4 40.8 %all-to-all-start = ((bf16[64,2,768]{2,1,0:T(2,128)(2,1)}), bf16[64,2,768]{2,1,0:T(2,128)(2,1)S(1)}, u32[]{:S(2)}, u32[]{:S(2)}) async-start(bf16[64,2,768]{2,1,0:T(2,128)(2,1)} %reshape.339), calls=%async_computation | async-start | bytes 393216 | tf_op jit(solution)/shard_map/all_to_all | solution.py:324
  22.7 22.7 %copy-start.3 = (bf16[1,256,384]{2,1,0:T(8,128)(2,1)S(1)}, bf16[1,256,384]{2,1,0:T(8,128)(2,1)}, u32[]{:S(2)}) copy-start(bf16[1,256,384]{2,1,0:T(8,128)(2,1)} %param.11) | copy-start | bytes 589828
  45.5 1.7 %copy-start.9 = (bf16[1,256,384]{1,2,0:T(8,128)(2,1)}, bf16[1,256,384]{1,2,0:T(8,128)(2,1)S(1)}, u32[]{:S(2)}) copy-start(bf16[1,256,384]{1,2,0:T(8,128)(2,1)S(1)} %copy.103) | copy-start | bytes 589828
  47.2 1.3 copy-start.12
  48.9 2.7 %copy-start.1 = (bf16[12,384,96]{2,1,0:T(8,128)(2,1)S(1)}, bf16[12,384,96]{2,1,0:T(8,128)(2,1)}, u32[]{:S(2)}) copy-start(bf16[12,384,96]{2,1,0:T(8,128)(2,1)} %gather_weights.1) | copy-start | bytes 2654212
  51.6 1.4 %copy-start.4 = (f32[256,4,4,96]{0,3,2,1:T(8,128)S(1)}, f32[256,4,4,96]{0,3,2,1:T(8,128)}, u32[]{:S(2)}) copy-start(f32[256,4,4,96]{0,3,2,1:T(8,128)} %copy.104) | copy-start | bytes 4718596
  59.4 1.5 %copy-start.5 = (f32[1,256,384]{2,1,0:T(8,128)S(1)}, f32[1,256,384]{2,1,0:T(8,128)}, u32[]{:S(2)}) copy-start(f32[1,256,384]{2,1,0:T(8,128)} %convert_element_type.92) | copy-start | bytes 1179652
  61.0 11.1 %copy-start.7 = (bf16[4,384,96]{1,2,0:T(8,128)(2,1)S(1)}, bf16[4,384,96]{1,2,0:T(8,128)(2,1)}, u32[]{:S(2)}) copy-start(bf16[4,384,96]{1,2,0:T(8,128)(2,1)} %convolution_convert_fusion.2) | copy-start | bytes 884740
  61.0 12.0 %copy-start.8 = (bf16[4,384,96]{1,2,0:T(8,128)(2,1)S(1)}, bf16[4,384,96]{1,2,0:T(8,128)(2,1)}, u32[]{:S(2)}) copy-start(bf16[4,384,96]{1,2,0:T(8,128)(2,1)} %convolution_convert_fusion.1) | copy-start | bytes 884740
  61.8 13.6 %copy-start.10 = (bf16[1,256,384]{1,2,0:T(8,128)(2,1)S(1)}, bf16[1,256,384]{1,2,0:T(8,128)(2,1)}, u32[]{:S(2)}) copy-start(bf16[1,256,384]{1,2,0:T(8,128)(2,1)} %copy-done.9) | copy-start | bytes 589828
  62.9 21.1 %all-to-all-start.1 = ((bf16[64,4,384]{2,1,0:T(4,128)(2,1)}), bf16[64,4,384]{2,1,0:T(4,128)(2,1)S(1)}, u32[]{:S(2)}, u32[]{:S(2)}) async-start(bf16[64,4,384]{2,1,0:T(4,128)(2,1)} %copy.112), calls=%async_computation.1 | async-start | bytes 393216 | tf_op jit(solution)/shard_map/all_to_all | solution.py:373
  73.0 11.0 %copy-start.16 = (f32[384]{0:T(512)S(1)}, f32[384]{0:T(512)}, u32[]{:S(2)}) copy-start(f32[384]{0:T(512)} %param.12) | copy-start | bytes 4612
  74.6 10.4 %copy-start.6 = (f32[1,256,384]{2,1,0:T(8,128)S(1)}, f32[1,256,384]{2,1,0:T(8,128)}, u32[]{:S(2)}) copy-start(f32[1,256,384]{2,1,0:T(8,128)} %copy.102) | copy-start | bytes 1179652

commit v2 on v1

--- a/solution.py
+++ b/solution.py
@@ -22,14 +22,69 @@
     return (x * 2 + yh, (z * 4 + yl) * 2 + c)
 
 
-def greet(peers):
+def greet(peers, others=0):
     barrier = pltpu.get_barrier_semaphore()
     for peer in peers:
         pl.semaphore_signal(barrier, inc=1, device_id=peer, device_id_type=MESH)
-    pl.semaphore_wait(barrier, len(peers))
-
-
-def gather_kernel(w_ref, out_ref, local_sem, send_sem, recv_sem):
+    pl.semaphore_wait(barrier, len(peers) + others)
+
+
+def line():
+    d, s, n = lax.axis_index("dp"), lax.axis_index("seq"), lax.axis_size("seq")
+    return d, s, n
+
+
+def greet_line():
+    d, s, n = line()
+    barrier = pltpu.get_barrier_semaphore()
+
+    def signal(k, carry):
+        pl.semaphore_signal(
+            barrier, inc=1, device_id=(d, (s + k) % n), device_id_type=MESH
+        )
+        return carry
+
+    lax.fori_loop(1, n, signal, 0)
+    return n - 1
+
+
+class Exchange:
+    def __init__(self, src, dst, local_sem, send_sem, recv_sem):
+        self.refs = (src, dst)
+        self.sems = (send_sem, recv_sem)
+        s = lax.axis_index("seq")
+        self.local = pltpu.make_async_copy(src.at[s], dst.at[s], local_sem)
+
+    def copy(self, k):
+        d, s, n = line()
+        peer = (s + k) % n
+        return pltpu.make_async_remote_copy(
+            self.refs[0].at[peer], self.refs[1].at[s],
+            self.sems[0].at[k - 1], self.sems[1].at[k - 1],
+            device_id=(d, peer), device_id_type=MESH,
+        )
+
+    def start(self):
+        def one(k, carry):
+            self.copy(k).start()
+            return carry
+
+        lax.fori_loop(1, line()[2], one, 0)
+        self.local.start()
+
+    def wait(self):
+        def one(k, carry):
+            self.copy(k).wait()
+            return carry
+
+        self.local.wait()
+        lax.fori_loop(1, line()[2], one, 0)
+
+
+def gather_kernel(
+    w_ref, mix_ref, out_ref, got_ref,
+    local_sem, send_sem, recv_sem, own_sem, line_send, line_recv,
+):
     x, yh, z, yl, c = place()
     pair = device(x, yh, z, yl, 1 - c)
     xs = [device((x + k) % 4, yh, z, yl, c) for k in (1, 2, 3)]
@@ -46,7 +101,7 @@
             src, dst, send_sem.at[sent], recv_sem.at[got], device_id=peer, device_id_type=MESH
         )
 
-    greet([pair] + xs + across)
+    greet(xs + across, greet_line())
     own = w_ref.at[pl.ds(half * c, half)]
     mine = part(x * 2 + yh)
     theirs = part(x * 2 + 1 - yh)
@@ -61,11 +116,13 @@
         for copy in over:
             copy.start()
 
-    local = pltpu.make_async_copy(own, mine, local_sem)
-    local.start()
     sends = [remote(own, mine, 2 + n, 1 + n, peer) for n, peer in enumerate(xs)]
     for copy in sends:
         copy.start()
+    exchange = Exchange(mix_ref, got_ref, own_sem, line_send, line_recv)
+    exchange.start()
+    local = pltpu.make_async_copy(own, mine, local_sem)
+    local.start()
     over[0].wait_recv()
     for n, peer in enumerate(xs):
         copy = remote(theirs, theirs, 5 + n, 4 + n, peer)
@@ -77,6 +134,7 @@
     whole = out_ref.at[pl.ds(half * c, half)]
     copy = remote(whole, whole, 8, 7, pair)
     copy.start()
+    exchange.wait()
     copy.wait_recv()
     for copy in sends + [copy]:
         copy.wait_send()
@@ -87,22 +145,34 @@
             copy.wait_send()
 
 
-def gather_weights(w):
+def line_semaphores(n):
+    return [
+        pltpu.SemaphoreType.DMA,
+        pltpu.SemaphoreType.DMA((n - 1,)),
+        pltpu.SemaphoreType.DMA((n - 1,)),
+    ]
+
+
+def gather_weights(w, mix):
     n, width, d = w.shape
+    vmem = pl.BlockSpec(memory_space=pltpu.VMEM)
     return pl.pallas_call(
         gather_kernel,
-        out_shape=jax.ShapeDtypeStruct((n, 8 * width, d), w.dtype),
-        in_specs=[pl.BlockSpec(memory_space=pltpu.VMEM)],
-        out_specs=pl.BlockSpec(memory_space=pltpu.VMEM),
+        out_shape=(
+            jax.ShapeDtypeStruct((n, 8 * width, d), w.dtype),
+            jax.ShapeDtypeStruct(mix.shape, mix.dtype),
+        ),
+        in_specs=[vmem] * 2,
+        out_specs=(vmem,) * 2,
         scratch_shapes=[
             pltpu.SemaphoreType.DMA,
             pltpu.SemaphoreType.DMA((9,)),
             pltpu.SemaphoreType.DMA((8,)),
-        ],
+        ]
+        + line_semaphores(mix.shape[0]),
         compiler_params=pltpu.CompilerParams(collective_id=1, has_side_effects=True),
-        cost_estimate=pl.CostEstimate(flops=0, bytes_accessed=40_000_000, transcendentals=0),
         name="gather_weights",
-    )(w)
+    )(w, mix)
 
 
 PIECES = (
@@ -115,11 +185,115 @@
 )
 
 
+class Sender:
+    def __init__(self, send_sem, recv_sem):
+        self.sems = (send_sem, recv_sem)
+        self.started = []
+
+    def __call__(self, src, dst, peer):
+        n = len(self.started)
+        copy = pltpu.make_async_remote_copy(
+            src, dst, self.sems[0].at[n], self.sems[1].at[n],
+            device_id=peer, device_id_type=MESH,
+        )
+        copy.start()
+        self.started.append(copy)
+        return copy
+
+    def finish(self):
+        for copy in self.started:
+            copy.wait_send()
+
+
+def landed(copies):
+    for copy in copies:
+        copy.wait_recv()
+
+
+def back_kernel(
+    mix_ref, gate_ref, up_ref, down_ref,
+    got_ref, out_ref,
+    wgot, xsend, xgot,
+    send_sem, recv_sem, own_sem, line_send, line_recv,
+):
+    x, yh, z, yl, c = place()
+    f32, bf16 = jnp.float32, jnp.bfloat16
+    pair = device(x, yh, z, yl, 1 - c)
+    xs = [device((x + k) % 4, yh, z, yl, c) for k in (1, 2, 3)]
+    greet(xs, greet_line())
+    send = Sender(send_sem, recv_sem)
+
+    grads = (gate_ref, up_ref, down_ref)
+    copies = [
+        send(ref.at[pl.ds(2 * (1 - c), 2)], wgot.at[kind], pair)
+        for kind, ref in enumerate(grads)
+    ]
+    exchange = Exchange(mix_ref, got_ref, own_sem, line_send, line_recv)
+    exchange.start()
+    for dest in range(4):
+        for h in range(2):
+            for q in range(4):
+                xsend[dest, h * 4 + q, :, 96:128] = jnp.zeros((REP, 32), bf16)
+            for q in (1, 3):
+                xsend[dest, h * 4 + q, 64:REP] = jnp.zeros((REP - 64, 128), bf16)
+    landed(copies)
+    for dest in range(4):
+        for h in range(2):
+            first = (dest * 2 + h) * 48
+            for i, pieces in enumerate(PIECES):
+                kind, k = divmod(i, 2)
+                for q, row, start, rows in pieces:
+                    at = slice(first + start, first + start + rows)
+                    total = grads[kind][2 * c + k, at, :].astype(f32)
+                    total = total + wgot[kind, k, at, :].astype(f32)
+                    xsend[dest, h * 4 + q, row : row + rows, 0:96] = total.astype(bf16)
+
+    copies = [
+        send(xsend.at[(x + k) % 4], xgot.at[k - 1], peer) for k, peer in zip((1, 2, 3), xs)
+    ]
+    exchange.wait()
+    landed(copies)
+
+    def add_x(n, carry):
+        total = xsend[x, n].astype(f32)
+        for k in range(3):
+            total = total + xgot[k, n].astype(f32)
+        out_ref[n] = total.astype(bf16)
+        return carry
+
+    lax.fori_loop(0, 8, add_x, 0)
+    send.finish()
+
+
+def exchange_back(mix, gate, up, down):
+    vmem = pl.BlockSpec(memory_space=pltpu.VMEM)
+    bf16 = jnp.bfloat16
+    return pl.pallas_call(
+        back_kernel,
+        out_shape=(
+            jax.ShapeDtypeStruct(mix.shape, mix.dtype),
+            jax.ShapeDtypeStruct((8, REP, 128), bf16),
+        ),
+        in_specs=[vmem] * 4,
+        out_specs=(vmem,) * 2,
+        scratch_shapes=[
+            pltpu.VMEM((3, 2, 384, 96), bf16),
+            pltpu.VMEM((4, 8, REP, 128), bf16),
+            pltpu.VMEM((3, 8, REP, 128), bf16),
+            pltpu.SemaphoreType.DMA((6,)),
+            pltpu.SemaphoreType.DMA((6,)),
+        ]
+        + line_semaphores(mix.shape[0]),
+        compiler_params=pltpu.CompilerParams(collective_id=3, has_side_effects=True),
+        name="exchange_back",
+    )(mix, gate, up, down)
+
+
 def sum_kernel(
     factor,
-    gate_ref, up_ref, down_ref, left_ref, right_ref, in_ref, outg_ref, norm_ref,
+    part_ref, left_ref, right_ref, in_ref, outg_ref, norm_ref,
     out_ref,
-    rep_ref, wgot, rgot, xsend, xgot, ysend, ygot, zall, yall, wother, repall,
+    rep_ref, rgot, ysend, ygot, zall, yall, wother, repall,
     send_sem, recv_sem,
 ):
     x, yh, z, yl, c = place()
@@ -131,27 +305,6 @@
     near = [device(x, yh, z, (yl + k) % 4, c) for k in (1, 2, 3)]
     far = [device(x, 1 - yh, z, (yl + k) % 4, c) for k in (0, 1, 2, 3)]
     zs = [device(x, yh, (z + k) % 8, yl, c) for k in range(1, 8)]
-    greet([pair] + xs + xo + near + far + zs)
-    started = []
-
-    def send(src, dst, peer):
-        n = len(started)
-        copy = pltpu.make_async_remote_copy(
-            src, dst, send_sem.at[n], recv_sem.at[n], device_id=peer, device_id_type=MESH
-        )
-        copy.start()
-        started.append(copy)
-        return copy
-
-    def landed(copies):
-        for copy in copies:
-            copy.wait_recv()
-
-    grads = (gate_ref, up_ref, down_ref)
-    copies = [
-        send(ref.at[pl.ds(2 * (1 - c), 2)], wgot.at[kind], pair)
-        for kind, ref in enumerate(grads)
-    ]
     for k in range(4):
         for n in range(8):
             row, lane = (k % 2) * 128 + n * 16, (k // 2) * 128
@@ -168,40 +321,20 @@
     ]
     gains.append(jnp.zeros((7, 128), f32))
     rep_ref[1, 0, 2] = jnp.concatenate(gains, axis=0).astype(bf16)
-    copies.append(send(rep_ref.at[1 - c], rgot, pair))
-    for dest in range(4):
-        for h in range(2):
-            for q in range(4):
-                xsend[dest, h * 4 + q, 0:REP, 96:128] = jnp.zeros((REP, 32), bf16)
-            for q in (1, 3):
-                xsend[dest, h * 4 + q, 64:REP] = jnp.zeros((REP - 64, 128), bf16)
+    greet([pair] + xs + xo + near + far + zs)
+    send = Sender(send_sem, recv_sem)
+
+    copies = [send(rep_ref.at[1 - c, x], rgot.at[0], pair)]
+    for k in (1, 2, 3):
+        copies.append(send(rep_ref.at[c, (x + k) % 4], rgot.at[k], xs[k - 1]))
+        copies.append(send(rep_ref.at[1 - c, (x + k) % 4], rgot.at[3 + k], xo[k - 1]))
+    for n in range(8):
+        ysend[n, 0:REP] = part_ref[n]
     landed(copies)
-    for dest in range(4):
-        for h in range(2):
-            first = (dest * 2 + h) * 48
-            for i, pieces in enumerate(PIECES):
-                kind, k = divmod(i, 2)
-                for q, row, start, rows in pieces:
-                    at = slice(first + start, first + start + rows)
-                    total = grads[kind][2 * c + k, at, :].astype(f32)
-                    total = total + wgot[kind, k, at, :].astype(f32)
-                    xsend[dest, h * 4 + q, row : row + rows, 0:96] = total.astype(bf16)
-        total = rep_ref[c, dest].astype(f32) + rgot[dest].astype(f32)
-        xsend[dest, :, REP:SLOT, :] = total.astype(bf16)
-
-    copies = [
-        send(xsend.at[(x + k) % 4], xgot.at[k - 1], peer) for k, peer in zip((1, 2, 3), xs)
-    ]
-    landed(copies)
-
-    def add_x(n, carry):
-        total = xsend[x, n].astype(f32)
-        for k in range(3):
-            total = total + xgot[k, n].astype(f32)
-        ysend[n] = total.astype(bf16)
-        return carry
-
-    lax.fori_loop(0, 8, add_x, 0)
+    total = rep_ref[c, x].astype(f32)
+    for k in range(7):
+        total = total + rgot[k].astype(f32)
+    ysend[:, REP:SLOT, :] = total.astype(bf16)
 
     copies = [
         send(ysend.at[yh * 4 + (yl + k) % 4], ygot.at[k - 1], peer)
@@ -257,14 +390,13 @@
         for t in range(3):
             row = value[3 * j + t : 3 * j + t + 1, :]
             out_ref[576 + j : 577 + j, t * 128 : t * 128 + 128] = row
-    for copy in started:
-        copy.wait_send()
+    send.finish()
 
 
 def sum_gradients(grads, factor):
     vmem = pl.BlockSpec(memory_space=pltpu.VMEM)
     bf16 = jnp.bfloat16
-    copies = 4 + 3 + 7 + 7 + 7 + 8
+    copies = 7 + 7 + 7 + 7 + 8
     return pl.pallas_call(
         functools.partial(sum_kernel, factor),
         out_shape=jax.ShapeDtypeStruct((584, 384), jnp.float32),
@@ -272,10 +404,7 @@
         out_specs=vmem,
         scratch_shapes=[
             pltpu.VMEM((2, 4, 8, 16, 128), bf16),
-            pltpu.VMEM((3, 2, 384, 96), bf16),
-            pltpu.VMEM((4, 8, 16, 128), bf16),
-            pltpu.VMEM((4, 8, SLOT, 128), bf16),
-            pltpu.VMEM((3, 8, SLOT, 128), bf16),
+            pltpu.VMEM((7, 8, 16, 128), bf16),
             pltpu.VMEM((8, SLOT, 128), bf16),
             pltpu.VMEM((7, SLOT, 128), bf16),
             pltpu.VMEM((8, SLOT, 128), bf16),
@@ -314,14 +443,16 @@
     block_hidden = data_count * shard_width
     quarter = block_hidden // nblocks
     packed = jnp.concatenate([gate_weight, up_weight, down_weight], axis=0).transpose(0, 2, 1)
-    weights = gather_weights(packed)
-    gate_full, up_full, down_full = weights[0:4], weights[4:8], weights[8:12]
     inputs = points[0].astype(jnp.float32)
     scaled = (inputs * in_gain).astype(jnp.bfloat16).reshape(blocks, block_size, channels)
     first_mix = jnp.einsum(
         "pb,abc->apc", left_factor, scaled, preferred_element_type=jnp.float32
     ).astype(jnp.bfloat16)
-    received = lax.all_to_all(first_mix, "seq", split_axis=1, concat_axis=0, tiled=True)
+    weights, received = gather_weights(
+        packed, first_mix.reshape(seq_count, block_size // seq_count, channels)
+    )
+    gate_full, up_full, down_full = weights[0:4], weights[4:8], weights[8:12]
+    down_grid = down_full.reshape(nblocks, nblocks, quarter, block_in)
     mixed = jnp.einsum("qa,apc->pqc", right_factor, received, preferred_element_type=jnp.float32)
     first_moved = received
     mixed = mixed.reshape(row_count, channels)
@@ -335,7 +466,6 @@
     act_gate = gate_pre * sig_gate
     hidden = (act_gate * up_pre).astype(jnp.bfloat16)
     hidden_grid = hidden.reshape(row_count, nblocks, nblocks, quarter)
-    down_grid = down_full.reshape(nblocks, nblocks, quarter, block_in)
     branch = jnp.einsum(
         "rkjf,jkfo->rjo", hidden_grid, down_grid, preferred_element_type=jnp.float32
     ).reshape(row_count, channels)
@@ -370,7 +500,13 @@
         "qa,pqc->apc", right_factor, dmixed, preferred_element_type=jnp.float32
     ).astype(jnp.bfloat16)
     grad_right = jnp.einsum("pqc,apc->qa", dmixed, first_moved, preferred_element_type=jnp.float32)
-    received = lax.all_to_all(dfirst, "seq", split_axis=0, concat_axis=1, tiled=True)
+    received, partial = exchange_back(
+        dfirst,
+        grad_gate.astype(jnp.bfloat16),
+        grad_up.astype(jnp.bfloat16),
+        grad_down.astype(jnp.bfloat16),
+    )
+    received = received.reshape(1, block_size, channels)
     dscaled = jnp.einsum("pb,apc->abc", left_factor, received, preferred_element_type=jnp.float32)
     grad_left = jnp.einsum("apc,abc->pb", received, scaled, preferred_element_type=jnp.float32)
     dscaled = dscaled.reshape(row_count, channels)
@@ -379,9 +515,7 @@
     factor = float(data_count * row_count * seq_count) ** (-0.5)
     sums = sum_gradients(
         (
-            grad_gate.astype(jnp.bfloat16),
-            grad_up.astype(jnp.bfloat16),
-            grad_down.astype(jnp.bfloat16),
+            partial,
             grad_left,
             grad_right,
             grad_in,

time: 139 us -> 124 us (0.89)
  starting transfers between devices: 24.6 us -> 0 us
  Pallas kernels: 65.4 us -> 88.4 us
  waiting for transfers between devices: 6.29 us -> 0 us
  local copies, waits for them, and re-layouts: 21.2 us -> 16.9 us
  other arithmetic: 6.15 us -> 4.06 us
    pallas_call x1 -> x2, Pallas kernels: 20 us -> 52.4 us  [the longest x1 31.6 us: gather_weights(): pl.pallas_call(gather_kernel, out_shape=(jax.ShapeDtypeStruct((n, 8 * wid...]
    all_to_all x2 -> x0, starting transfers between devices: 24.6 us -> none  [the longest x1 15.4 us: shards(): lax.all_to_all(first_mix, 'seq', split_axis=1, concat_axis=0, tiled=True)]
    pallas_call x1, Pallas kernels: 45.5 us -> 36 us  [sum_gradients(): pl.pallas_call(functools.partial(sum_kernel, factor), out_shape=jax.Shape...]
    all_to_all x2 -> x0, waiting for transfers between devices: 6.29 us -> none  [the longest x1 6.29 us: shards(): lax.all_to_all(dfirst, 'seq', split_axis=0, concat_axis=1, tiled=True)]
    unnamed x1 -> x0, other arithmetic: 1.8 us -> none
    unnamed x40 -> x38, local copies, waits for them, and re-layouts: 3.61 us -> 2.18 us
  transfers between devices with their start and end apart: 2 -> 0, of which waited for: 1 -> 0; matrix products, arithmetic and copies ran while one was open for 8% -> 0% of each run, Pallas kernels for 14% -> 0%
where the time goes in v2:
time: 124 us; the launch traced here: 123 us
  Pallas kernels  88.4 us (71%)
  local copies, waits for them, and re-layouts  16.9 us (14%)
  matrix products  13.2 us (11%)
  other arithmetic  4.06 us (3%)
    pallas_call x1, Pallas kernels, sum_gradients(): pl.pallas_call(functools.partial(sum_kernel, factor), out_shape=jax.Shape...  36 us
    pallas_call x1, Pallas kernels, gather_weights(): pl.pallas_call(gather_kernel, out_shape=(jax.ShapeDtypeStruct((n, 8 * wid...  31.6 us
    pallas_call x1, Pallas kernels, exchange_back(): pl.pallas_call(back_kernel, out_shape=(jax.ShapeDtypeStruct(mix.shape, mi...  20.8 us

profile of v2, /device:TPU:1, one launch (start us, length us, event | category | flops | bytes accessed | tf_op | source)
XLA Modules:
  0.0 123.4 jit_solution(3446119577402890902)
XLA Ops:
  0.7 0.8 mul.192
  1.5 1.5 %maximum_bitcast_fusion.w_ref = bf16[12,48,96]{2,1,0:T(8,128)(2,1)} fusion(bf16[4,96,48]{1,2,0:T(8,128)(2,1)} %param.19, bf16[4,96,48]{1,2,0:T(8,128)(2,1)} %param.18, bf16[4,96,48]{1,2,0:T(8,128)(2,1)} %param.17), kind=kLoop, calls=%fused_computation.53 | loop fusion | flops 110592 | bytes 221184 | tf_op jit(solution)/shard_map/transpose | solution.py:445
  3.1 1.1 fusion.9
  4.2 0.7 reshape.310.mix_ref
  4.9 31.6 %gather_weights.1 = (bf16[12,384,96]{2,1,0:T(8,128)(2,1)}, bf16[64,4,384]{2,1,0:T(4,128)(2,1)}) custom-call(bf16[12,48,96]{2,1,0:T(8,128)(2,1)} %maximum_bitcast_fusion.w_ref, bf16[64,4,384]{2,1,0:T(4,128)(2,1)} %reshape.310.mix_ref), custom_call_target="tpu_custom_call" | custom-call | tf_op jit(solution)/shard_map/gather_weights/pallas_call | solution.py:159
  36.6 1.1 fusion.22
  38.7 0.9 multiply_convert_fusion.1
  40.8 1.9 %fusion.3 = (bf16[256,4,384]{0,2,1:T(8,128)(2,1)S(1)}, bf16[256,4,384]{0,2,1:T(8,128)(2,1)S(1)}, bf16[256,4,384]{0,2,1:T(8,128)(2,1)}) fusion(f32[256,4,4,96]{0,3,2,1:T(8,128)S(1)} %copy.78, f32[4,384,256]{2,1,0:T(8,128)S(1)} %fusion.30, bf16[12,384,96]{2,1,0:T(8,128)(2,1)S(1)} %copy-done.1, bf16[256,4,96]{0,2,1:T(8,128)(2,1)S(1)} %get-tuple-element.25), kind=kOutput, calls=%fused_computation.5 | convolution fusion | flops 81395712 | bytes 6586368 | tf_op jit(solution)/shard_map/rkd,kfd->rkf/dot_general | solution.py:463
  43.1 0.9 copy-done.10
  44.0 0.4 multiply_reduce_fusion
  44.4 0.9 copy.83
  45.3 1.4 %fusion.11 = f32[4,96,256,1]{2,1,3,0:T(8,128)S(1)} fusion(bf16[4,4,96,96]{3,2,1,0:T(8,128)(2,1)S(1)} %bitcast.155, bf16[256,4,4,96]{0,3,2,1:T(8,128)(2,1)} %bitcast.162), kind=kOutput, calls=%fused_computation.25 | convolution fusion | flops 75497472 | bytes 1474560 | tf_op jit(solution)/shard_map/rkjf,jkfo->rjo/dot_general | solution.py:469
  46.8 0.9 copy.76
  48.5 0.8 multiply_reduce_fusion.1
  49.5 0.8 copy.116
  50.3 0.4 convolution_convert_fusion.2
  50.7 0.9 copy.90.gate_ref
  51.6 0.4 convolution_convert_fusion.1
  52.0 1.0 copy.91.up_ref
  53.0 2.3 %convolution_convert_fusion = bf16[4,4,96,96]{3,2,1,0:T(8,128)(2,1)} fusion(bf16[256,4,96,1]{0,2,3,1:T(8,128)(2,1)S(1)} %bitcast.161, bf16[256,4,4,96]{0,3,2,1:T(8,128)(2,1)} %bitcast.163), kind=kOutput, calls=%fused_computation.16 | convolution fusion | flops 75644928 | bytes 1277952 | tf_op jit(solution)/shard_map/rjo,rkjf->jkfo/dot_general | solution.py:477
  55.3 20.8 %exchange_back.1 = (bf16[64,4,384]{2,1,0:T(4,128)(2,1)}, bf16[8,80,128]{2,1,0:T(8,128)(2,1)}) custom-call(bf16[64,4,384]{2,1,0:T(4,128)(2,1)} %bitcast.164, bf16[4,384,96]{2,1,0:T(8,128)(2,1)} %copy.90.gate_ref, bf16[4,384,96]{2,1,0:T(8,128)(2,1)} %copy.91.up_ref, bf16[4,384,96]{2,1,0:T(8,128)(2,1)} %bitcast.165), custom_call_target="tpu_custom_call" | custom-call | tf_op jit(solution)/shard_map/exchange_back/pallas_call | solution.py:271
  76.1 1.0 reshape.320
  77.1 1.0 fusion.19
  78.2 1.0 fusion.24.left_ref
  79.1 0.8 convolution_bitcast_fusion.1.right_ref
  80.0 0.6 fusion.13.in_ref
  80.6 0.7 reduce_sum.52.norm_ref
  81.3 36.0 %sum_gradients.1 = f32[584,384]{1,0:T(8,128)} custom-call(bf16[8,80,128]{2,1,0:T(8,128)(2,1)} %get-tuple-element.17.part_ref, f32[256,256]{1,0:T(8,128)} %fusion.24.left_ref, f32[64,64]{1,0:T(8,128)} %convolution_bitcast_fusion.1.right_ref, f32[384]{0:T(512)} %fusion.13.in_ref, f32[384]{0:T(512)} %get-tuple-element.23.outg_ref, f32[384]{0:T(512)} %reduce_sum.52.norm_ref), custom_call_target="tpu_custom_call" | custom-call | tf_op jit(solution)/shard_map/sum_gradients/pallas_call | solution.py:400
  117.3 1.7 %slice.36 = f32[256,256]{1,0:T(8,128)} slice(f32[584,384]{1,0:T(8,128)} %sum_gradients.1), slice={[0:256], [0:256]} | slice | bytes 524288 | tf_op jit(solution)/shard_map/slice | solution.py:535
  118.9 1.4 %slice.37 = f32[64,64]{1,0:T(8,128)} slice(f32[584,384]{1,0:T(8,128)} %sum_gradients.1), slice={[256:320], [0:64]} | slice | bytes 32768 | tf_op jit(solution)/shard_map/slice | solution.py:536
  120.3 1.4 %slice_reduce_fusion = (f32[384]{0:T(512)}, f32[384]{0:T(512)}, f32[384]{0:T(512)}) fusion(f32[584,384]{1,0:T(8,128)} %sum_gradients.1), kind=kLoop, calls=%fused_computation.56 | loop fusion | bytes 9216 | tf_op jit(solution)/shard_map/slice | solution.py:539
  121.7 1.7 %fusion.29 = (f32[192,96]{1,0:T(8,128)}, f32[192,96]{1,0:T(8,128)}, f32[192,96]{1,0:T(8,128)}) fusion(f32[584,384]{1,0:T(8,128)} %sum_gradients.1), kind=kLoop, calls=%fused_computation.61 | loop fusion | bytes 442368 | tf_op jit(solution)/shard_map/slice | solution.py:529
  (54 shorter events, 3.4 us)
Async XLA Ops:
  0.6 2.4 %copy-start = (bf16[256,256]{1,0:T(8,128)(2,1)S(1)}, bf16[256,256]{1,0:T(8,128)(2,1)}, u32[]{:S(2)}) copy-start(bf16[256,256]{1,0:T(8,128)(2,1)} %param.14) | copy-start | bytes 393220
  0.7 37.0 %copy-start.2 = (bf16[1,256,384]{2,1,0:T(8,128)(2,1)S(1)}, bf16[1,256,384]{2,1,0:T(8,128)(2,1)}, u32[]{:S(2)}) copy-start(bf16[1,256,384]{2,1,0:T(8,128)(2,1)} %param.10) | copy-start | bytes 589828
  0.7 35.9 %copy-start.15 = (bf16[64,64]{1,0:T(8,128)(2,1)S(1)}, bf16[64,64]{1,0:T(8,128)(2,1)}, u32[]{:S(2)}) copy-start(bf16[64,64]{1,0:T(8,128)(2,1)} %param.15) | copy-start | bytes 24580
  0.7 37.0 %copy-start.14 = (f32[384]{0:T(512)S(1)}, f32[384]{0:T(512)}, u32[]{:S(2)}) copy-start(f32[384]{0:T(512)} %param.13) | copy-start | bytes 4612
  38.0 1.6 %copy-start.1 = (bf16[12,384,96]{2,1,0:T(8,128)(2,1)S(1)}, bf16[12,384,96]{2,1,0:T(8,128)(2,1)}, u32[]{:S(2)}) copy-start(bf16[12,384,96]{2,1,0:T(8,128)(2,1)} %get-tuple-element.15) | copy-start | bytes 2654212
  38.3 1.3 %copy-start.7 = (bf16[1,256,384]{2,1,0:T(8,128)(2,1)S(1)}, bf16[1,256,384]{2,1,0:T(8,128)(2,1)}, u32[]{:S(2)}) copy-start(bf16[1,256,384]{2,1,0:T(8,128)(2,1)} %param.11) | copy-start | bytes 589828
  39.8 0.7 copy-start.11
  42.7 1.7 %copy-start.3 = (bf16[256,4,384]{0,2,1:T(8,128)(2,1)}, bf16[256,4,384]{0,2,1:T(8,128)(2,1)S(1)}, u32[]{:S(2)}) copy-start(bf16[256,4,384]{0,2,1:T(8,128)(2,1)S(1)} %get-tuple-element.28) | copy-start | bytes 2359300
  42.7 1.7 %copy-start.5 = (bf16[256,4,384]{0,2,1:T(8,128)(2,1)}, bf16[256,4,384]{0,2,1:T(8,128)(2,1)S(1)}, u32[]{:S(2)}) copy-start(bf16[256,4,384]{0,2,1:T(8,128)(2,1)S(1)} %get-tuple-element.27) | copy-start | bytes 2359300
  42.7 1.3 %copy-start.10 = (f32[256,4,96]{0,2,1:T(8,128)S(1)}, f32[256,4,96]{0,2,1:T(8,128)}, u32[]{:S(2)}) copy-start(f32[256,4,96]{0,2,1:T(8,128)} %get-tuple-element.26) | copy-start | bytes 1179652
  46.8 1.7 %copy-start.17 = (f32[384]{0:T(512)S(1)}, f32[384]{0:T(512)}, u32[]{:S(2)}) copy-start(f32[384]{0:T(512)} %param.16) | copy-start | bytes 4612
  48.4 2.0 %copy-start.4 = (bf16[256,4,384]{0,2,1:T(8,128)(2,1)S(1)}, bf16[256,4,384]{0,2,1:T(8,128)(2,1)}, u32[]{:S(2)}) copy-start(bf16[256,4,384]{0,2,1:T(8,128)(2,1)} %copy-done.3) | copy-start | bytes 2359300
  49.3 2.4 %copy-start.6 = (bf16[256,4,384]{0,2,1:T(8,128)(2,1)S(1)}, bf16[256,4,384]{0,2,1:T(8,128)(2,1)}, u32[]{:S(2)}) copy-start(bf16[256,4,384]{0,2,1:T(8,128)(2,1)} %copy-done.5) | copy-start | bytes 2359300
  51.6 1.3 %copy-start.12 = (bf16[1,256,384]{1,2,0:T(8,128)(2,1)S(1)}, bf16[1,256,384]{1,2,0:T(8,128)(2,1)}, u32[]{:S(2)}) copy-start(bf16[1,256,384]{1,2,0:T(8,128)(2,1)} %copy-done.11) | copy-start | bytes 589828
  53.0 24.1 %copy-start.8 = (f32[1,256,384]{2,1,0:T(8,128)S(1)}, f32[1,256,384]{2,1,0:T(8,128)}, u32[]{:S(2)}) copy-start(f32[1,256,384]{2,1,0:T(8,128)} %copy.83) | copy-start | bytes 1179652
  53.0 24.1 %copy-start.9 = (f32[1,256,384]{2,1,0:T(8,128)S(1)}, f32[1,256,384]{2,1,0:T(8,128)}, u32[]{:S(2)}) copy-start(f32[1,256,384]{2,1,0:T(8,128)} %copy.76) | copy-start | bytes 1179652
  53.0 24.1 %copy-start.16 = (f32[384]{0:T(512)S(1)}, f32[384]{0:T(512)}, u32[]{:S(2)}) copy-start(f32[384]{0:T(512)} %param.12) | copy-start | bytes 4612
  77.1 2.0 %copy-start.13 = (bf16[64,4,384]{2,1,0:T(4,128)(2,1)S(1)}, bf16[64,4,384]{2,1,0:T(4,128)(2,1)}, u32[]{:S(2)}) copy-start(bf16[64,4,384]{2,1,0:T(4,128)(2,1)} %get-tuple-element.14) | copy-start | bytes 589828

commit v3 on v2

--- a/solution.py
+++ b/solution.py
@@ -8,8 +8,7 @@
 from jax.sharding import PartitionSpec as P
 
 MESH = pl.DeviceIdType.MESH
-SLOT = 96
-REP = 80
+ROWS = 80
 
 
 def place():
@@ -233,9 +232,9 @@
     for dest in range(4):
         for h in range(2):
             for q in range(4):
-                xsend[dest, h * 4 + q, :, 96:128] = jnp.zeros((REP, 32), bf16)
+                xsend[dest, h * 4 + q, :, 96:128] = jnp.zeros((ROWS, 32), bf16)
             for q in (1, 3):
-                xsend[dest, h * 4 + q, 64:REP] = jnp.zeros((REP - 64, 128), bf16)
+                xsend[dest, h * 4 + q, 64:ROWS] = jnp.zeros((ROWS - 64, 128), bf16)
     landed(copies)
     for dest in range(4):
         for h in range(2):
@@ -272,14 +271,14 @@
         back_kernel,
         out_shape=(
             jax.ShapeDtypeStruct(mix.shape, mix.dtype),
-            jax.ShapeDtypeStruct((8, REP, 128), bf16),
+            jax.ShapeDtypeStruct((8, ROWS, 128), bf16),
         ),
         in_specs=[vmem] * 4,
         out_specs=(vmem,) * 2,
         scratch_shapes=[
             pltpu.VMEM((3, 2, 384, 96), bf16),
-            pltpu.VMEM((4, 8, REP, 128), bf16),
-            pltpu.VMEM((3, 8, REP, 128), bf16),
+            pltpu.VMEM((4, 8, ROWS, 128), bf16),
+            pltpu.VMEM((3, 8, ROWS, 128), bf16),
             pltpu.SemaphoreType.DMA((6,)),
             pltpu.SemaphoreType.DMA((6,)),
         ]
@@ -293,7 +292,7 @@
     factor,
     part_ref, left_ref, right_ref, in_ref, outg_ref, norm_ref,
     out_ref,
-    rep_ref, rgot, ysend, ygot, zall, yall, wother, repall,
+    rep_ref, rgot, ysend, ygot, zall, yall, repall, wgot, wzall, wyall, wother,
     send_sem, recv_sem,
 ):
     x, yh, z, yl, c = place()
@@ -328,54 +327,63 @@
     for k in (1, 2, 3):
         copies.append(send(rep_ref.at[c, (x + k) % 4], rgot.at[k], xs[k - 1]))
         copies.append(send(rep_ref.at[1 - c, (x + k) % 4], rgot.at[3 + k], xo[k - 1]))
-    for n in range(8):
-        ysend[n, 0:REP] = part_ref[n]
+
+    def along_y(src, dst):
+        sent = [
+            send(src.at[yh * 4 + (yl + k) % 4], dst.at[k - 1], peer)
+            for k, peer in zip((1, 2, 3), near)
+        ]
+        return sent + [
+            send(src.at[(1 - yh) * 4 + (yl + k) % 4], dst.at[3 + k], peer)
+            for k, peer in zip((0, 1, 2, 3), far)
+        ]
+
+    def add(first, others):
+        total = first.astype(f32)
+        for k in range(others.shape[0]):
+            total = total + others[k].astype(f32)
+        return total.astype(bf16)
+
+    def add_all(parts):
+        total = parts[0].astype(f32)
+        for k in range(1, 8):
+            total = total + parts[k].astype(f32)
+        return total.astype(bf16)
+
+    w_y = along_y(part_ref, wgot)
     landed(copies)
-    total = rep_ref[c, x].astype(f32)
-    for k in range(7):
-        total = total + rgot[k].astype(f32)
-    ysend[:, REP:SLOT, :] = total.astype(bf16)
-
-    copies = [
-        send(ysend.at[yh * 4 + (yl + k) % 4], ygot.at[k - 1], peer)
-        for k, peer in zip((1, 2, 3), near)
-    ]
-    copies += [
-        send(ysend.at[(1 - yh) * 4 + (yl + k) % 4], ygot.at[3 + k], peer)
-        for k, peer in zip((0, 1, 2, 3), far)
-    ]
-    landed(copies)
-    total = ysend[y].astype(f32)
-    for k in range(7):
-        total = total + ygot[k].astype(f32)
-    zall[z] = total.astype(bf16)
-
-    landed([send(zall.at[z], zall.at[z], peer) for peer in zs])
-    total = zall[0].astype(f32)
-    for k in range(1, 8):
-        total = total + zall[k].astype(f32)
-    yall[y] = total.astype(bf16)
-
-    copies = [send(yall.at[y], yall.at[y], peer) for peer in near]
-    tail = yall.at[y, REP:SLOT]
-    copies += [send(tail, tail, peer) for peer in far]
-    landed(copies)
-    copies = [send(yall.at[pl.ds(4 * yh, 4)], wother, pair)]
-    tails = yall.at[:, REP:SLOT]
-    copies += [send(tails, repall.at[c, x], peer) for peer in [pair] + xs + xo]
-    repall[c, x] = yall[:, REP:SLOT, :]
+    ysend[...] = add(rep_ref[c, x], rgot)
+    r_y = along_y(ysend, ygot)
+    landed(w_y)
+    wzall[z] = add(part_ref[y], wgot)
+    w_z = [send(wzall.at[z], wzall.at[z], peer) for peer in zs]
+    landed(r_y)
+    zall[z] = add(ysend[y], ygot)
+    r_z = [send(zall.at[z], zall.at[z], peer) for peer in zs]
+    landed(r_z)
+    yall[y] = add_all(zall)
+    r_back = [send(yall.at[y], yall.at[y], peer) for peer in near + far]
+    landed(w_z)
+    wyall[yl] = add_all(wzall)
+    w_back = [send(wyall.at[yl], wyall.at[yl], peer) for peer in near]
+    landed(r_back)
+    copies = [send(yall, repall.at[c, x], peer) for peer in [pair] + xs + xo]
+    repall[c, x] = yall[...]
+    landed(w_back)
+    w_pair = send(wyall, wother, pair)
 
     def unpack(chunk, core):
         for i, pieces in enumerate(PIECES):
             kind, k = divmod(i, 2)
             for q, row, start, rows in pieces:
                 at = pl.multiple_of(kind * 192 + (2 * core + k) * 48 + start, 16)
-                value = chunk(q)[row : row + rows, 0:96].astype(f32) * factor
+                value = chunk[q, row : row + rows, 0:96].astype(f32) * factor
                 out_ref[pl.ds(at, rows), 256:352] = value
 
-    unpack(lambda q: yall.at[4 * yh + q], c)
+    unpack(wyall, c)
+    landed([w_pair])
+    unpack(wother, 1 - c)
     landed(copies)
-    unpack(lambda q: wother.at[q], 1 - c)
     for k in range(4):
         for n in range(8):
             row, lane = (k % 2) * 128 + n * 16, (k // 2) * 128
@@ -396,7 +404,7 @@
 def sum_gradients(grads, factor):
     vmem = pl.BlockSpec(memory_space=pltpu.VMEM)
     bf16 = jnp.bfloat16
-    copies = 7 + 7 + 7 + 7 + 8
+    copies = 7 * 7 + 3 + 1
     return pl.pallas_call(
         functools.partial(sum_kernel, factor),
         out_shape=jax.ShapeDtypeStruct((584, 384), jnp.float32),
@@ -405,18 +413,46 @@
         scratch_shapes=[
             pltpu.VMEM((2, 4, 8, 16, 128), bf16),
             pltpu.VMEM((7, 8, 16, 128), bf16),
-            pltpu.VMEM((8, SLOT, 128), bf16),
-            pltpu.VMEM((7, SLOT, 128), bf16),
-            pltpu.VMEM((8, SLOT, 128), bf16),
-            pltpu.VMEM((8, SLOT, 128), bf16),
-            pltpu.VMEM((4, SLOT, 128), bf16),
+            pltpu.VMEM((8, 16, 128), bf16),
+            pltpu.VMEM((7, 16, 128), bf16),
+            pltpu.VMEM((8, 16, 128), bf16),
+            pltpu.VMEM((8, 16, 128), bf16),
             pltpu.VMEM((2, 4, 8, 16, 128), bf16),
+            pltpu.VMEM((7, ROWS, 128), bf16),
+            pltpu.VMEM((8, ROWS, 128), bf16),
+            pltpu.VMEM((4, ROWS, 128), bf16),
+            pltpu.VMEM((4, ROWS, 128), bf16),
             pltpu.SemaphoreType.DMA((copies,)),
             pltpu.SemaphoreType.DMA((copies,)),
         ],
         compiler_params=pltpu.CompilerParams(collective_id=2, has_side_effects=True),
         name="sum_gradients",
     )(*grads)
+
+
+def split_kernel(sums_ref, left, right, gain_in, gain_out, norm, gate, up, down):
+    left[...] = sums_ref[0:256, 0:256]
+    right[...] = sums_ref[256:320, 0:64]
+    for j, ref in enumerate((gain_in, gain_out, norm)):
+        for t in range(3):
+            row = sums_ref[576 + j : 577 + j, 128 * t : 128 * t + 128]
+            ref[128 * t : 128 * t + 128] = row.reshape(128)
+    for j, ref in enumerate((gate, up, down)):
+        for k in range(4):
+            at = 192 * j + 48 * k
+            ref[k] = sums_ref[at : at + 48, 256:352]
+
+
+def split_sums(sums):
+    vmem = pl.BlockSpec(memory_space=pltpu.VMEM)
+    shapes = [(256, 256), (64, 64)] + [(384,)] * 3 + [(4, 48, 96)] * 3
+    return pl.pallas_call(
+        split_kernel,
+        out_shape=[jax.ShapeDtypeStruct(shape, jnp.float32) for shape in shapes],
+        in_specs=[vmem],
+        out_specs=[vmem] * len(shapes),
+        name="split_sums",
+    )(sums)
 
 
 def shards(
@@ -525,21 +561,16 @@
         factor,
     )
 
-    def weight(n):
-        part = sums[192 * n : 192 * n + 192, 256:352]
-        return part.reshape(nblocks, shard_width, block_in).transpose(0, 2, 1)
-
+    left_sum, right_sum, in_sum, out_sum, norm_sum, *w_sums = split_sums(sums)
     return (
         layer_out[None],
         grad_points[None],
-        sums[0:256, 0:256],
-        sums[256:320, 0:64],
-        sums[576],
-        sums[577],
-        sums[578],
-        weight(0),
-        weight(1),
-        weight(2),
+        left_sum,
+        right_sum,
+        in_sum,
+        out_sum,
+        norm_sum,
+        *(w_sum.transpose(0, 2, 1) for w_sum in w_sums),
     )
 
 

time: 124 us -> 116 us (0.935)
  local copies, waits for them, and re-layouts: 16.9 us -> 11.1 us
  Pallas kernels: 88.4 us -> 85.1 us
    slice x4 -> x0, local copies, waits for them, and re-layouts: 6.17 us -> none  [the longest x1 1.7 us: weight(): part = sums[192 * n:192 * n + 192, 256:352]]
    pallas_call x1, Pallas kernels: 36 us -> 30.7 us  [sum_gradients(): pl.pallas_call(functools.partial(sum_kernel, factor), out_shape=jax.Shape...]
    pallas_call x0 -> x1, Pallas kernels: none -> 1.99 us  [split_sums(): pl.pallas_call(split_kernel, out_shape=[jax.ShapeDtypeStruct(shape, jnp.f...]
where the time goes in v3:
time: 116 us; the launch traced here: 115 us
  Pallas kernels  85.1 us (73%)
  matrix products  13.9 us (12%)
  local copies, waits for them, and re-layouts  11.1 us (10%)
  other arithmetic  4.32 us (4%)
    pallas_call x1, Pallas kernels, gather_weights(): pl.pallas_call(gather_kernel, out_shape=(jax.ShapeDtypeStruct((n, 8 * wid...  31.6 us
    pallas_call x1, Pallas kernels, sum_gradients(): pl.pallas_call(functools.partial(sum_kernel, factor), out_shape=jax.Shape...  30.7 us
    pallas_call x1, Pallas kernels, exchange_back(): pl.pallas_call(back_kernel, out_shape=(jax.ShapeDtypeStruct(mix.shape, mi...  20.8 us

profile of v3, /device:TPU:1, one launch (start us, length us, event | category | flops | bytes accessed | tf_op | source)
XLA Modules:
  0.0 115.3 jit_solution(7687139963585275254)
XLA Ops:
  0.7 0.8 mul.192
  1.5 1.5 %maximum_bitcast_fusion.w_ref = bf16[12,48,96]{2,1,0:T(8,128)(2,1)} fusion(bf16[4,96,48]{1,2,0:T(8,128)(2,1)} %param.19, bf16[4,96,48]{1,2,0:T(8,128)(2,1)} %param.18, bf16[4,96,48]{1,2,0:T(8,128)(2,1)} %param.17), kind=kLoop, calls=%fused_computation.53 | loop fusion | flops 110592 | bytes 221184 | tf_op jit(solution)/shard_map/transpose | solution.py:481
  3.1 1.1 fusion.9
  4.2 0.7 reshape.301.mix_ref
  4.9 31.6 %gather_weights.1 = (bf16[12,384,96]{2,1,0:T(8,128)(2,1)}, bf16[64,4,384]{2,1,0:T(4,128)(2,1)}) custom-call(bf16[12,48,96]{2,1,0:T(8,128)(2,1)} %maximum_bitcast_fusion.w_ref, bf16[64,4,384]{2,1,0:T(4,128)(2,1)} %reshape.301.mix_ref), custom_call_target="tpu_custom_call" | custom-call | tf_op jit(solution)/shard_map/gather_weights/pallas_call | solution.py:158
  36.6 1.1 fusion.22
  37.8 0.9 copy.70
  38.8 0.3 reshape.304
  39.4 1.2 %multiply_convert_fusion.1 = (bf16[256,4,96]{0,2,1:T(8,128)(2,1)S(1)}, f32[256,4,96]{0,2,1:T(8,128)S(1)}) fusion(f32[4,96]{1,0:T(4,128)S(1)} %mul.192, f32[256]{0:T(256)S(1)} %add_rsqrt_fusion, f32[256,4,96]{0,2,1:T(8,128)} %bitcast.152, f32[256,4,96]{0,2,1:T(8,128)S(1)} %copy.71, f32[4,96]{1,0:T(4,128)S(1)} %mul.184), kind=kLoop, calls=%fused_computation.44 | loop fusion | flops 491520 | bytes 1380352 | tf_op jit(solution)/shard_map/convert_element_type | solution.py:498
  40.8 0.3 convolution_bitcast_fusion
  41.5 0.4 fusion.29
  41.8 1.9 %fusion.3 = (bf16[256,4,384]{0,2,1:T(8,128)(2,1)S(1)}, bf16[256,4,384]{0,2,1:T(8,128)(2,1)S(1)}, bf16[256,4,384]{0,2,1:T(8,128)(2,1)}) fusion(f32[256,4,4,96]{0,3,2,1:T(8,128)S(1)} %copy.78, f32[4,384,256]{2,1,0:T(8,128)S(1)} %fusion.29, bf16[12,384,96]{2,1,0:T(8,128)(2,1)S(1)} %copy-done.1, bf16[256,4,96]{0,2,1:T(8,128)(2,1)S(1)} %get-tuple-element.38), kind=kOutput, calls=%fused_computation.5 | convolution fusion | flops 81395712 | bytes 6586368 | tf_op jit(solution)/shard_map/rkd,kfd->rkf/dot_general | solution.py:499
  43.7 0.3 fusion.30
  44.1 0.4 multiply_reduce_fusion
  45.1 1.5 %fusion.11 = f32[4,96,256,1]{2,1,3,0:T(8,128)S(1)} fusion(bf16[4,4,96,96]{3,2,1,0:T(8,128)(2,1)S(1)} %bitcast.149, bf16[256,4,4,96]{0,3,2,1:T(8,128)(2,1)} %bitcast.156), kind=kOutput, calls=%fused_computation.25 | convolution fusion | flops 75497472 | bytes 1474560 | tf_op jit(solution)/shard_map/rkjf,jkfo->rjo/dot_general | solution.py:505
  46.5 0.9 copy.76
  48.2 0.8 multiply_reduce_fusion.1
  49.2 0.8 copy.116
  50.0 1.1 convolution_convert_fusion.2
  51.2 1.9 %copy.90.gate_ref = bf16[4,384,96]{2,1,0:T(8,128)(2,1)} copy(bf16[4,384,96]{1,2,0:T(8,128)(2,1)} %convolution_convert_fusion.2) | data formatting | bytes 589824 | tf_op jit(solution)/shard_map/convert_element_type | solution.py:541
  53.1 0.4 convolution_convert_fusion.1
  53.4 0.9 copy.91.up_ref
  54.4 2.3 %convolution_convert_fusion = bf16[4,4,96,96]{3,2,1,0:T(8,128)(2,1)} fusion(bf16[256,4,96,1]{0,2,3,1:T(8,128)(2,1)S(1)} %bitcast.155, bf16[256,4,4,96]{0,3,2,1:T(8,128)(2,1)} %bitcast.157), kind=kOutput, calls=%fused_computation.16 | convolution fusion | flops 75644928 | bytes 1277952 | tf_op jit(solution)/shard_map/rjo,rkjf->jkfo/dot_general | solution.py:513
  56.7 20.8 %exchange_back.1 = (bf16[64,4,384]{2,1,0:T(4,128)(2,1)}, bf16[8,80,128]{2,1,0:T(8,128)(2,1)}) custom-call(bf16[64,4,384]{2,1,0:T(4,128)(2,1)} %bitcast.158, bf16[4,384,96]{2,1,0:T(8,128)(2,1)} %copy.90.gate_ref, bf16[4,384,96]{2,1,0:T(8,128)(2,1)} %copy.91.up_ref, bf16[4,384,96]{2,1,0:T(8,128)(2,1)} %bitcast.159), custom_call_target="tpu_custom_call" | custom-call | tf_op jit(solution)/shard_map/exchange_back/pallas_call | solution.py:270
  77.5 1.0 reshape.311
  78.5 1.0 fusion.19
  79.6 1.0 fusion.24.left_ref
  80.5 0.8 convolution_bitcast_fusion.1.right_ref
  81.3 0.6 fusion.13.in_ref
  82.0 0.7 reduce_sum.52.norm_ref
  82.7 30.7 %sum_gradients.1.sums_ref = f32[584,384]{1,0:T(8,128)} custom-call(bf16[8,80,128]{2,1,0:T(8,128)(2,1)} %get-tuple-element.25.part_ref, f32[256,256]{1,0:T(8,128)} %fusion.24.left_ref, f32[64,64]{1,0:T(8,128)} %convolution_bitcast_fusion.1.right_ref, f32[384]{0:T(512)} %fusion.13.in_ref, f32[384]{0:T(512)} %get-tuple-element.36.outg_ref, f32[384]{0:T(512)} %reduce_sum.52.norm_ref), custom_call_target="tpu_custom_call" | custom-call | tf_op jit(solution)/shard_map/sum_gradients/pallas_call | solution.py:408
  113.3 2.0 %split_sums.1 = (f32[256,256]{1,0:T(8,128)}, f32[64,64]{1,0:T(8,128)}, f32[384]{0:T(512)}, f32[384]{0:T(512)}, f32[384]{0:T(512)}, /*index=5*/f32[4,48,96]{2,1,0...) custom-call(f32[584,384]{1,0:T(8,128)} %sum_gradients.1.sums_ref), custom_call_target="tpu_custom_call" | custom-call | tf_op jit(solution)/shard_map/split_sums/pallas_call | solution.py:449
  (47 shorter events, 2.5 us)
Async XLA Ops:
  0.6 2.4 %copy-start = (bf16[256,256]{1,0:T(8,128)(2,1)S(1)}, bf16[256,256]{1,0:T(8,128)(2,1)}, u32[]{:S(2)}) copy-start(bf16[256,256]{1,0:T(8,128)(2,1)} %param.14) | copy-start | bytes 393220
  0.7 37.0 %copy-start.2 = (bf16[1,256,384]{2,1,0:T(8,128)(2,1)S(1)}, bf16[1,256,384]{2,1,0:T(8,128)(2,1)}, u32[]{:S(2)}) copy-start(bf16[1,256,384]{2,1,0:T(8,128)(2,1)} %param.10) | copy-start | bytes 589828
  0.7 35.9 %copy-start.13 = (bf16[64,64]{1,0:T(8,128)(2,1)S(1)}, bf16[64,64]{1,0:T(8,128)(2,1)}, u32[]{:S(2)}) copy-start(bf16[64,64]{1,0:T(8,128)(2,1)} %param.15) | copy-start | bytes 24580
  0.7 37.0 %copy-start.12 = (f32[384]{0:T(512)S(1)}, f32[384]{0:T(512)}, u32[]{:S(2)}) copy-start(f32[384]{0:T(512)} %param.13) | copy-start | bytes 4612
  38.8 1.8 %copy-start.1 = (bf16[12,384,96]{2,1,0:T(8,128)(2,1)S(1)}, bf16[12,384,96]{2,1,0:T(8,128)(2,1)}, u32[]{:S(2)}) copy-start(bf16[12,384,96]{2,1,0:T(8,128)(2,1)} %get-tuple-element.23) | copy-start | bytes 2654212
  39.1 1.5 %copy-start.7 = (bf16[1,256,384]{2,1,0:T(8,128)(2,1)S(1)}, bf16[1,256,384]{2,1,0:T(8,128)(2,1)}, u32[]{:S(2)}) copy-start(bf16[1,256,384]{2,1,0:T(8,128)(2,1)} %param.11) | copy-start | bytes 589828
  40.8 0.7 copy-start.9
  43.7 0.9 copy-start.3
  43.7 1.2 %copy-start.5 = (bf16[256,4,384]{0,2,1:T(8,128)(2,1)}, bf16[256,4,384]{0,2,1:T(8,128)(2,1)S(1)}, u32[]{:S(2)}) copy-start(bf16[256,4,384]{0,2,1:T(8,128)(2,1)S(1)} %get-tuple-element.40) | copy-start | bytes 2359300
  46.5 1.6 %copy-start.15 = (f32[384]{0:T(512)S(1)}, f32[384]{0:T(512)}, u32[]{:S(2)}) copy-start(f32[384]{0:T(512)} %param.16) | copy-start | bytes 4612
  48.1 2.0 %copy-start.4 = (bf16[256,4,384]{0,2,1:T(8,128)(2,1)S(1)}, bf16[256,4,384]{0,2,1:T(8,128)(2,1)}, u32[]{:S(2)}) copy-start(bf16[256,4,384]{0,2,1:T(8,128)(2,1)} %copy-done.3) | copy-start | bytes 2359300
  49.0 4.1 %copy-start.6 = (bf16[256,4,384]{0,2,1:T(8,128)(2,1)S(1)}, bf16[256,4,384]{0,2,1:T(8,128)(2,1)}, u32[]{:S(2)}) copy-start(bf16[256,4,384]{0,2,1:T(8,128)(2,1)} %copy-done.5) | copy-start | bytes 2359300
  51.2 3.2 %copy-start.10 = (bf16[1,256,384]{1,2,0:T(8,128)(2,1)S(1)}, bf16[1,256,384]{1,2,0:T(8,128)(2,1)}, u32[]{:S(2)}) copy-start(bf16[1,256,384]{1,2,0:T(8,128)(2,1)} %copy-done.9) | copy-start | bytes 589828
  54.4 24.1 %copy-start.8 = (f32[1,256,384]{2,1,0:T(8,128)S(1)}, f32[1,256,384]{2,1,0:T(8,128)}, u32[]{:S(2)}) copy-start(f32[1,256,384]{2,1,0:T(8,128)} %copy.76) | copy-start | bytes 1179652
  54.4 24.1 %copy-start.14 = (f32[384]{0:T(512)S(1)}, f32[384]{0:T(512)}, u32[]{:S(2)}) copy-start(f32[384]{0:T(512)} %param.12) | copy-start | bytes 4612
  78.5 2.0 %copy-start.11 = (bf16[64,4,384]{2,1,0:T(4,128)(2,1)S(1)}, bf16[64,4,384]{2,1,0:T(4,128)(2,1)}, u32[]{:S(2)}) copy-start(bf16[64,4,384]{2,1,0:T(4,128)(2,1)} %get-tuple-element.22) | copy-start | bytes 589828

commit v4 on v3

--- a/solution.py
+++ b/solution.py
@@ -21,11 +21,19 @@
     return (x * 2 + yh, (z * 4 + yl) * 2 + c)
 
 
-def greet(peers, others=0):
+def signal(peers):
     barrier = pltpu.get_barrier_semaphore()
     for peer in peers:
         pl.semaphore_signal(barrier, inc=1, device_id=peer, device_id_type=MESH)
-    pl.semaphore_wait(barrier, len(peers) + others)
+
+
+def await_all(count):
+    pl.semaphore_wait(pltpu.get_barrier_semaphore(), count)
+
+
+def greet(peers, others=0):
+    signal(peers)
+    await_all(len(peers) + others)
 
 
 def line():
@@ -37,13 +45,13 @@
     d, s, n = line()
     barrier = pltpu.get_barrier_semaphore()
 
-    def signal(k, carry):
+    def one(k, carry):
         pl.semaphore_signal(
             barrier, inc=1, device_id=(d, (s + k) % n), device_id_type=MESH
         )
         return carry
 
-    lax.fori_loop(1, n, signal, 0)
+    lax.fori_loop(1, n, one, 0)
     return n - 1
 
 
@@ -210,17 +218,37 @@
 
 
 def back_kernel(
-    mix_ref, gate_ref, up_ref, down_ref,
+    mix_ref, dgate_ref, dupper_ref, hidden_ref, input_ref, cotangent_ref,
     got_ref, out_ref,
-    wgot, xsend, xgot,
+    gate_ref, up_ref, down_ref, wgot, xsend, xgot,
     send_sem, recv_sem, own_sem, line_send, line_recv,
 ):
     x, yh, z, yl, c = place()
     f32, bf16 = jnp.float32, jnp.bfloat16
     pair = device(x, yh, z, yl, 1 - c)
     xs = [device((x + k) % 4, yh, z, yl, c) for k in (1, 2, 3)]
-    greet(xs, greet_line())
+    signal(xs)
+    others = greet_line()
     send = Sender(send_sem, recv_sem)
+    side = input_ref.shape[1]
+
+    def product(a, b):
+        dims = (((1,), (1,)), ((), ()))
+        return lax.dot_general(a, b, dims, preferred_element_type=f32).astype(bf16)
+
+    def multiply(core):
+        for i in range(2):
+            k = 2 * core + i
+            gate_ref[k] = product(dgate_ref[k], input_ref[k])
+            up_ref[k] = product(dupper_ref[k], input_ref[k])
+            at = pl.ds(pl.multiple_of(k * side, 16), side)
+            for n in range(4):
+                down_ref[k, n * side : (n + 1) * side] = product(
+                    hidden_ref[n, at, :], cotangent_ref[k]
+                )
+
+    multiply(1 - c)
+    await_all(len(xs) + others)
 
     grads = (gate_ref, up_ref, down_ref)
     copies = [
@@ -229,6 +257,7 @@
     ]
     exchange = Exchange(mix_ref, got_ref, own_sem, line_send, line_recv)
     exchange.start()
+    multiply(c)
     for dest in range(4):
         for h in range(2):
             for q in range(4):
@@ -264,7 +293,7 @@
     send.finish()
 
 
-def exchange_back(mix, gate, up, down):
+def exchange_back(mix, dgate, dupper, hidden, hidden_in, cotangent):
     vmem = pl.BlockSpec(memory_space=pltpu.VMEM)
     bf16 = jnp.bfloat16
     return pl.pallas_call(
@@ -273,9 +302,12 @@
             jax.ShapeDtypeStruct(mix.shape, mix.dtype),
             jax.ShapeDtypeStruct((8, ROWS, 128), bf16),
         ),
-        in_specs=[vmem] * 4,
+        in_specs=[vmem] * 6,
         out_specs=(vmem,) * 2,
         scratch_shapes=[
+            pltpu.VMEM((4, 384, 96), bf16),
+            pltpu.VMEM((4, 384, 96), bf16),
+            pltpu.VMEM((4, 384, 96), bf16),
             pltpu.VMEM((3, 2, 384, 96), bf16),
             pltpu.VMEM((4, 8, ROWS, 128), bf16),
             pltpu.VMEM((3, 8, ROWS, 128), bf16),
@@ -285,7 +317,7 @@
         + line_semaphores(mix.shape[0]),
         compiler_params=pltpu.CompilerParams(collective_id=3, has_side_effects=True),
         name="exchange_back",
-    )(mix, gate, up, down)
+    )(mix, dgate, dupper, hidden, hidden_in, cotangent)
 
 
 def sum_kernel(
@@ -304,6 +336,8 @@
     near = [device(x, yh, z, (yl + k) % 4, c) for k in (1, 2, 3)]
     far = [device(x, 1 - yh, z, (yl + k) % 4, c) for k in (0, 1, 2, 3)]
     zs = [device(x, yh, (z + k) % 8, yl, c) for k in range(1, 8)]
+    peers = [pair] + xs + xo + near + far + zs
+    signal(peers)
     for k in range(4):
         for n in range(8):
             row, lane = (k % 2) * 128 + n * 16, (k // 2) * 128
@@ -320,7 +354,7 @@
     ]
     gains.append(jnp.zeros((7, 128), f32))
     rep_ref[1, 0, 2] = jnp.concatenate(gains, axis=0).astype(bf16)
-    greet([pair] + xs + xo + near + far + zs)
+    await_all(len(peers))
     send = Sender(send_sem, recv_sem)
 
     copies = [send(rep_ref.at[1 - c, x], rgot.at[0], pair)]
@@ -510,17 +544,12 @@
     dhidden = jnp.einsum(
         "rjo,jkfo->rkjf", grad_grid, down_grid, preferred_element_type=jnp.float32
     ).reshape(row_count, nblocks, block_hidden)
-    grad_down = jnp.einsum(
-        "rjo,rkjf->jkfo", grad_grid, hidden_grid, preferred_element_type=jnp.float32
-    ).reshape(nblocks, block_hidden, block_in)
     dgate = (dhidden * up_pre * sig_gate * (1.0 + gate_pre * (1.0 - sig_gate))).astype(jnp.bfloat16)
     dupper = (dhidden * act_gate).astype(jnp.bfloat16)
     dhid_in = jnp.einsum("rkf,kfd->rkd", dgate, gate_full, preferred_element_type=jnp.float32)
     dhid_in = (
         dhid_in + jnp.einsum("rkf,kfd->rkd", dupper, up_full, preferred_element_type=jnp.float32)
     ).reshape(row_count, channels)
-    grad_gate = jnp.einsum("rkd,rkf->kfd", hidden_in, dgate, preferred_element_type=jnp.float32)
-    grad_up = jnp.einsum("rkd,rkf->kfd", hidden_in, dupper, preferred_element_type=jnp.float32)
     grad_norm = jnp.sum(dhid_in * normed, axis=0)
     scaled_grad = dhid_in * norm_gain
     dresid = cotangent[0].astype(jnp.float32) + inv_rms * (
@@ -538,9 +567,11 @@
     grad_right = jnp.einsum("pqc,apc->qa", dmixed, first_moved, preferred_element_type=jnp.float32)
     received, partial = exchange_back(
         dfirst,
-        grad_gate.astype(jnp.bfloat16),
-        grad_up.astype(jnp.bfloat16),
-        grad_down.astype(jnp.bfloat16),
+        dgate.transpose(1, 2, 0),
+        dupper.transpose(1, 2, 0),
+        hidden.transpose(1, 2, 0),
+        hidden_in.transpose(1, 2, 0),
+        grad_grid.transpose(1, 2, 0),
     )
     received = received.reshape(1, block_size, channels)
     dscaled = jnp.einsum("pb,apc->abc", left_factor, received, preferred_element_type=jnp.float32)

time: 116 us -> 119 us (1.026)
  other arithmetic: 4.32 us -> 7.47 us
  matrix products: 13.9 us -> 12.5 us
  local copies, waits for them, and re-layouts: 11.1 us -> 12.5 us
    dot_general x3 -> x0, matrix products: 3.77 us -> none  [the longest x1 2.31 us: shards(): jnp.einsum('rjo,rkjf->jkfo', grad_grid, hidden_grid, preferred_element_ty...]
    convert_element_type x2 -> x0, local copies, waits for them, and re-layouts: 2.86 us -> none  [the longest x1 1.92 us: shards(): grad_gate.astype(jnp.bfloat16)]
    reshape x2, local copies, waits for them, and re-layouts: 0.42 us -> 2.92 us  [shards(): dhid_in = (dhid_in + jnp.einsum('rkf,kfd->rkd', dupper, up_full, preferre...]
    unnamed x34 -> x38, local copies, waits for them, and re-layouts: 1.64 us -> 3.46 us
    convert_element_type x0 -> x1, other arithmetic: none -> 1.37 us  [shards(): hidden = (act_gate * up_pre).astype(jnp.bfloat16)]
    reduce_sum x1, other arithmetic: 0.79 us -> 2.01 us  [shards(): grad_out = jnp.sum(dresid * mixed, axis=0)]
where the time goes in v4:
time: 119 us
  Pallas kernels  85.5 us (72%)
  local copies, waits for them, and re-layouts  12.5 us (11%)
  matrix products  12.5 us (11%)
  other arithmetic  7.47 us (6%)
    pallas_call x1, Pallas kernels, gather_weights(): pl.pallas_call(gather_kernel, out_shape=(jax.ShapeDtypeStruct((n, 8 * wid...  31.5 us
    pallas_call x1, Pallas kernels, sum_gradients(): pl.pallas_call(functools.partial(sum_kernel, factor), out_shape=jax.Shape...  30.5 us
    pallas_call x1, Pallas kernels, exchange_back(): pl.pallas_call(back_kernel, out_shape=(jax.ShapeDtypeStruct(mix.shape, mi...  21.4 us
    unnamed x38, local copies, waits for them, and re-layouts  3.46 us
    reshape x2, local copies, waits for them, and re-layouts, shards(): dhid_in = (dhid_in + jnp.einsum('rkf,kfd->rkd', dupper, up_full, preferre...  2.92 us

profile of v4, /device:TPU:1, one launch (start us, length us, event | category | flops | bytes accessed | tf_op | source)
XLA Modules:
  0.0 118.9 jit_solution(10687604003392475852)
XLA Ops:
  0.7 0.8 mul.198
  1.5 1.5 %maximum_bitcast_fusion.w_ref = bf16[12,48,96]{2,1,0:T(8,128)(2,1)} fusion(bf16[4,96,48]{1,2,0:T(8,128)(2,1)} %param.19, bf16[4,96,48]{1,2,0:T(8,128)(2,1)} %param.18, bf16[4,96,48]{1,2,0:T(8,128)(2,1)} %param.17), kind=kLoop, calls=%fused_computation.50 | loop fusion | flops 110592 | bytes 221184 | tf_op jit(solution)/shard_map/transpose | solution.py:515
  3.1 1.1 fusion.9
  4.2 0.7 reshape.299.mix_ref
  4.9 31.5 %gather_weights.1 = (bf16[12,384,96]{2,1,0:T(8,128)(2,1)}, bf16[64,4,384]{2,1,0:T(4,128)(2,1)}) custom-call(bf16[12,48,96]{2,1,0:T(8,128)(2,1)} %maximum_bitcast_fusion.w_ref, bf16[64,4,384]{2,1,0:T(4,128)(2,1)} %reshape.299.mix_ref), custom_call_target="tpu_custom_call" | custom-call | tf_op jit(solution)/shard_map/gather_weights/pallas_call | solution.py:166
  36.5 1.1 fusion.21
  38.6 1.0 multiply_convert_fusion.2
  39.6 0.8 slice.9
  40.4 0.8 copy.47
  41.2 1.4 %convolution_bitcast_fusion = f32[256,4,4,96]{0,3,1,2:T(8,128)S(1)} fusion(bf16[4,4,96,96]{3,2,1,0:T(8,128)(2,1)} %bitcast.147, bf16[256,4,96,1]{0,2,3,1:T(8,128)(2,1)} %bitcast.152), kind=kOutput, calls=%fused_computation.16 | convolution fusion | flops 75497472 | bytes 2064384 | tf_op jit(solution)/shard_map/rjo,jkfo->rkjf/dot_general | solution.py:544
  42.7 0.8 copy-done.6
  43.5 0.4 fusion.28
  43.9 2.4 %fusion.3 = (bf16[256,4,384]{0,2,1:T(8,128)(2,1)S(1)}, bf16[256,4,384]{0,2,1:T(8,128)(2,1)S(1)}, bf16[256,4,384]{0,2,1:T(8,128)(2,1)}, f32[4,384,256]{2,1,0:T(8,128)}) fusion(f32[256,4,4,96]{0,3,2,1:T(8,128)S(1)} %copy.48, f32[4,384,256]{2,1,0:T(8,128)S(1)} %fusion.28, bf16[12,384,96]{2,1,0:T(8,128)(2,1)S(1)} %copy-done.1, bf16[256,4,96]{0,2,1:T(8,128)(2,1)S(1)} %copy-done.6), kind=kOutput, calls=%fused_computation.5 | convolution fusion | flops 81395712 | bytes 8159232 | tf_op jit(solution)/shard_map/rkd,kfd->rkf/dot_general | solution.py:533
  46.6 0.9 copy-done.12
  47.5 1.1 multiply_reduce_fusion
  48.6 1.9 %copy.53 = f32[1,256,384]{2,1,0:T(8,128)} copy(f32[1,256,384]{1,2,0:T(8,128)} %bitcast.145) | data formatting | bytes 786432 | tf_op jit(solution)/shard_map/reshape | solution.py:552
  50.5 1.6 %fusion.10 = f32[4,96,256,1]{2,1,3,0:T(8,128)S(1)} fusion(bf16[4,4,96,96]{3,2,1,0:T(8,128)(2,1)} %bitcast.148, bf16[256,4,4,96]{0,3,2,1:T(8,128)(2,1)} %bitcast.159), kind=kOutput, calls=%fused_computation.22 | convolution fusion | flops 75497472 | bytes 1474560 | tf_op jit(solution)/shard_map/rkjf,jkfo->rjo/dot_general | solution.py:539
  52.2 0.9 copy.46
  53.2 0.8 convert_element_type.83
  54.2 1.0 reshape.308
  55.3 2.0 %multiply_reduce_fusion.1 = (f32[384]{0:T(512)}, f32[4,64,384]{2,1,0:T(8,128)S(1)}) fusion(f32[4,384,64]{1,2,0:T(8,128)S(1)} %fusion.21, f32[4,64]{1,0:T(4,128)S(1)} %div.17, f32[4,64,384]{2,1,0:T(8,128)} %bitcast.155, f32[384]{0:T(512)S(1)} %copy-done.14, f32[4,64,384]{2,1,0:T(8,128)} %reshape.308, f32[384]{0:T(512)S(1)} %copy-done.17, ...), kind=kLoop, calls=%fused_computation.36 | loop fusion | flops 1080960 | bytes 1776128 | tf_op jit(solution)/shard_map/reduce_sum | solution.py:558
  57.6 0.8 copy.77
  58.4 1.4 %multiply_convert_fusion.hidden_ref = bf16[4,384,256]{2,1,0:T(8,128)(2,1)} fusion(f32[4,384,256]{2,1,0:T(8,128)S(1)} %fusion.28, f32[4,384,256]{2,1,0:T(8,128)S(1)} %copy-done.9), kind=kLoop, calls=%fused_computation.15 | loop fusion | flops 2359296 | bytes 3932160 | tf_op jit(solution)/shard_map/convert_element_type | solution.py:537
  59.8 21.4 %exchange_back.1 = (bf16[64,4,384]{2,1,0:T(4,128)(2,1)}, bf16[8,80,128]{2,1,0:T(8,128)(2,1)}) custom-call(bf16[64,4,384]{2,1,0:T(4,128)(2,1)} %bitcast.158, bf16[4,384,256]{2,1,0:T(8,128)(2,1)} %bitcast.149, bf16[4,384,256]{2,1,0:T(8,128)(2,1)} %bitcast.150, bf16[4,384,256]{2,1,0:T(8,128)(2,1)} %multiply_convert_fusion.hidden_ref, ...), custom_call_target="tpu_custom_call" | custom-call | tf_op jit(solution)/shard_map/exchange_back/pallas_call | solution.py:299
  81.2 1.0 reshape.309
  82.2 1.0 fusion.18
  83.3 1.0 fusion.23.left_ref
  84.2 0.8 convolution_bitcast_fusion.1.right_ref
  85.0 0.6 fusion.12.in_ref
  85.7 0.7 reduce_sum.52.norm_ref
  86.4 30.5 %sum_gradients.1.sums_ref = f32[584,384]{1,0:T(8,128)} custom-call(bf16[8,80,128]{2,1,0:T(8,128)(2,1)} %get-tuple-element.25.part_ref, f32[256,256]{1,0:T(8,128)} %fusion.23.left_ref, f32[64,64]{1,0:T(8,128)} %convolution_bitcast_fusion.1.right_ref, f32[384]{0:T(512)} %fusion.12.in_ref, f32[384]{0:T(512)} %get-tuple-element.36.outg_ref, f32[384]{0:T(512)} %reduce_sum.52.norm_ref), custom_call_target="tpu_custom_call" | custom-call | tf_op jit(solution)/shard_map/sum_gradients/pallas_call | solution.py:442
  116.9 2.0 %split_sums.1 = (f32[256,256]{1,0:T(8,128)}, f32[64,64]{1,0:T(8,128)}, f32[384]{0:T(512)}, f32[384]{0:T(512)}, f32[384]{0:T(512)}, /*index=5*/f32[4,48,96]{2,1,0...) custom-call(f32[584,384]{1,0:T(8,128)} %sum_gradients.1.sums_ref), custom_call_target="tpu_custom_call" | custom-call | tf_op jit(solution)/shard_map/split_sums/pallas_call | solution.py:483
  (47 shorter events, 2.1 us)
Async XLA Ops:
  0.6 2.4 %copy-start = (bf16[256,256]{1,0:T(8,128)(2,1)S(1)}, bf16[256,256]{1,0:T(8,128)(2,1)}, u32[]{:S(2)}) copy-start(bf16[256,256]{1,0:T(8,128)(2,1)} %param.14) | copy-start | bytes 393220
  0.7 37.0 %copy-start.2 = (bf16[1,256,384]{2,1,0:T(8,128)(2,1)S(1)}, bf16[1,256,384]{2,1,0:T(8,128)(2,1)}, u32[]{:S(2)}) copy-start(bf16[1,256,384]{2,1,0:T(8,128)(2,1)} %param.10) | copy-start | bytes 589828
  0.7 35.8 %copy-start.15 = (bf16[64,64]{1,0:T(8,128)(2,1)S(1)}, bf16[64,64]{1,0:T(8,128)(2,1)}, u32[]{:S(2)}) copy-start(bf16[64,64]{1,0:T(8,128)(2,1)} %param.15) | copy-start | bytes 24580
  0.7 37.0 %copy-start.14 = (f32[384]{0:T(512)S(1)}, f32[384]{0:T(512)}, u32[]{:S(2)}) copy-start(f32[384]{0:T(512)} %param.13) | copy-start | bytes 4612
  37.9 1.6 %copy-start.1 = (bf16[12,384,96]{2,1,0:T(8,128)(2,1)S(1)}, bf16[12,384,96]{2,1,0:T(8,128)(2,1)}, u32[]{:S(2)}) copy-start(bf16[12,384,96]{2,1,0:T(8,128)(2,1)} %get-tuple-element.23) | copy-start | bytes 2654212
  38.3 2.1 %copy-start.7 = (bf16[1,256,384]{2,1,0:T(8,128)(2,1)S(1)}, bf16[1,256,384]{2,1,0:T(8,128)(2,1)}, u32[]{:S(2)}) copy-start(bf16[1,256,384]{2,1,0:T(8,128)(2,1)} %param.11) | copy-start | bytes 589828
  42.6 0.9 copy-start.6
  46.2 2.4 %copy-start.4 = (bf16[256,4,384]{0,2,1:T(8,128)(2,1)}, bf16[256,4,384]{0,2,1:T(8,128)(2,1)S(1)}, u32[]{:S(2)}) copy-start(bf16[256,4,384]{0,2,1:T(8,128)(2,1)S(1)} %get-tuple-element.41) | copy-start | bytes 2359300
  46.2 2.4 %copy-start.5 = (bf16[256,4,384]{0,2,1:T(8,128)(2,1)}, bf16[256,4,384]{0,2,1:T(8,128)(2,1)S(1)}, u32[]{:S(2)}) copy-start(bf16[256,4,384]{0,2,1:T(8,128)(2,1)S(1)} %get-tuple-element.40) | copy-start | bytes 2359300
  46.2 1.3 %copy-start.12 = (f32[256,4,96]{0,2,1:T(8,128)S(1)}, f32[256,4,96]{0,2,1:T(8,128)}, u32[]{:S(2)}) copy-start(f32[256,4,96]{0,2,1:T(8,128)} %get-tuple-element.39) | copy-start | bytes 1179652
  50.5 3.4 %copy-start.3 = (f32[4,96,256]{2,1,0:T(8,128)S(1)}, f32[4,96,256]{2,1,0:T(8,128)}, u32[]{:S(2)}) copy-start(f32[4,96,256]{2,1,0:T(8,128)} %get-tuple-element.46) | copy-start | bytes 1179652
  52.1 3.1 %copy-start.8 = (bf16[1,256,384]{2,1,0:T(8,128)(2,1)S(1)}, bf16[1,256,384]{2,1,0:T(8,128)(2,1)}, u32[]{:S(2)}) copy-start(bf16[1,256,384]{2,1,0:T(8,128)(2,1)} %param.11) | copy-start | bytes 589828
  52.2 3.1 %copy-start.17 = (f32[384]{0:T(512)S(1)}, f32[384]{0:T(512)}, u32[]{:S(2)}) copy-start(f32[384]{0:T(512)} %param.16) | copy-start | bytes 4612
  55.3 3.1 %copy-start.9 = (f32[4,384,256]{2,1,0:T(8,128)S(1)}, f32[4,384,256]{2,1,0:T(8,128)}, u32[]{:S(2)}) copy-start(f32[4,384,256]{2,1,0:T(8,128)} %get-tuple-element.45) | copy-start | bytes 4718596
  59.8 22.4 %copy-start.10 = (f32[1,256,384]{2,1,0:T(8,128)S(1)}, f32[1,256,384]{2,1,0:T(8,128)}, u32[]{:S(2)}) copy-start(f32[1,256,384]{2,1,0:T(8,128)} %copy.53) | copy-start | bytes 1179652
  59.8 22.4 %copy-start.11 = (f32[1,256,384]{2,1,0:T(8,128)S(1)}, f32[1,256,384]{2,1,0:T(8,128)}, u32[]{:S(2)}) copy-start(f32[1,256,384]{2,1,0:T(8,128)} %copy.46) | copy-start | bytes 1179652
  59.8 22.4 %copy-start.16 = (f32[384]{0:T(512)S(1)}, f32[384]{0:T(512)}, u32[]{:S(2)}) copy-start(f32[384]{0:T(512)} %param.12) | copy-start | bytes 4612
  82.2 2.0 %copy-start.13 = (bf16[64,4,384]{2,1,0:T(4,128)(2,1)S(1)}, bf16[64,4,384]{2,1,0:T(4,128)(2,1)}, u32[]{:S(2)}) copy-start(bf16[64,4,384]{2,1,0:T(4,128)(2,1)} %get-tuple-element.22) | copy-start | bytes 589828

commit v5 on v4

--- a/solution.py
+++ b/solution.py
@@ -177,7 +177,9 @@
             pltpu.SemaphoreType.DMA((8,)),
         ]
         + line_semaphores(mix.shape[0]),
-        compiler_params=pltpu.CompilerParams(collective_id=1, has_side_effects=True),
+        compiler_params=pltpu.CompilerParams(
+            collective_id=1, has_side_effects=True, vmem_limit_bytes=8 << 20
+        ),
         name="gather_weights",
     )(w, mix)
 
@@ -315,7 +317,9 @@
             pltpu.SemaphoreType.DMA((6,)),
         ]
         + line_semaphores(mix.shape[0]),
-        compiler_params=pltpu.CompilerParams(collective_id=3, has_side_effects=True),
+        compiler_params=pltpu.CompilerParams(
+            collective_id=3, has_side_effects=True, vmem_limit_bytes=16 << 20
+        ),
         name="exchange_back",
     )(mix, dgate, dupper, hidden, hidden_in, cotangent)
 
@@ -459,7 +463,9 @@
             pltpu.SemaphoreType.DMA((copies,)),
             pltpu.SemaphoreType.DMA((copies,)),
         ],
-        compiler_params=pltpu.CompilerParams(collective_id=2, has_side_effects=True),
+        compiler_params=pltpu.CompilerParams(
+            collective_id=2, has_side_effects=True, vmem_limit_bytes=8 << 20
+        ),
         name="sum_gradients",
     )(*grads)
 
@@ -485,6 +491,7 @@
         out_shape=[jax.ShapeDtypeStruct(shape, jnp.float32) for shape in shapes],
         in_specs=[vmem],
         out_specs=[vmem] * len(shapes),
+        compiler_params=pltpu.CompilerParams(vmem_limit_bytes=8 << 20),
         name="split_sums",
     )(sums)
 

time: 119 us -> 110 us (0.924)
  Pallas kernels: 85.5 us -> 78.7 us
  other arithmetic: 7.47 us -> 6.18 us
    pallas_call x1, Pallas kernels: 21.4 us -> 19.2 us  [exchange_back(): pl.pallas_call(back_kernel, out_shape=(jax.ShapeDtypeStruct(mix.shape, mi...]
    pallas_call x1, Pallas kernels: 30.5 us -> 28.7 us  [sum_gradients(): pl.pallas_call(functools.partial(sum_kernel, factor), out_shape=jax.Shape...]
    pallas_call x1, Pallas kernels: 31.5 us -> 29.9 us  [gather_weights(): pl.pallas_call(gather_kernel, out_shape=(jax.ShapeDtypeStruct((n, 8 * wid...]
    unnamed x38 -> x36, local copies, waits for them, and re-layouts: 3.46 us -> 1.98 us
    dot_general x1, matrix products: 1.04 us -> 2.29 us  [shards(): jnp.einsum('pb,apc->abc', left_factor, received, preferred_element_type=j...]
where the time goes in v5:
time: 110 us
  Pallas kernels  78.7 us (72%)
  matrix products  12.2 us (11%)
  local copies, waits for them, and re-layouts  11.9 us (11%)
  other arithmetic  6.18 us (6%)
    pallas_call x1, Pallas kernels, gather_weights(): pl.pallas_call(gather_kernel, out_shape=(jax.ShapeDtypeStruct((n, 8 * wid...  29.9 us
    pallas_call x1, Pallas kernels, sum_gradients(): pl.pallas_call(functools.partial(sum_kernel, factor), out_shape=jax.Shape...  28.7 us
    pallas_call x1, Pallas kernels, exchange_back(): pl.pallas_call(back_kernel, out_shape=(jax.ShapeDtypeStruct(mix.shape, mi...  19.2 us
    reshape x2, local copies, waits for them, and re-layouts, shards(): dhid_in = (dhid_in + jnp.einsum('rkf,kfd->rkd', dupper, up_full, preferre...  4.03 us
    dot_general x1, matrix products, shards(): jnp.einsum('rkjf,jkfo->rjo', hidden_grid, down_grid, preferred_element_ty...  2.38 us
    dot_general x1, matrix products, shards(): jnp.einsum('rkd,kfd->rkf', hidden_in, gate_full, preferred_element_type=j...  2.34 us
    dot_general x1, matrix products, shards(): jnp.einsum('pb,apc->abc', left_factor, received, preferred_element_type=j...  2.29 us

profile of v5, /device:TPU:1, one launch (start us, length us, event | category | flops | bytes accessed | tf_op | source)
XLA Modules:
  0.0 109.8 jit_solution(14433956654012440971)
XLA Ops:
  0.7 0.8 mul.198
  1.5 0.9 maximum_bitcast_fusion.w_ref
  2.4 1.2 %fusion.9 = bf16[1,256,384]{2,1,0:T(8,128)(2,1)S(1)} fusion(bf16[256,256]{1,0:T(8,128)(2,1)S(1)} %copy-done, bf16[1,256,384]{2,1,0:T(8,128)(2,1)} %param.10, f32[384]{0:T(512)} %param.12), kind=kOutput, calls=%fused_computation.20 | convolution fusion | flops 50724864 | bytes 525824 | tf_op jit(solution)/shard_map/pb,abc->apc/dot_general | solution.py:525
  3.6 29.9 %gather_weights.1 = (bf16[12,384,96]{2,1,0:T(8,128)(2,1)S(1)}, bf16[64,4,384]{2,1,0:T(4,128)(2,1)S(1)}) custom-call(bf16[12,48,96]{2,1,0:T(8,128)(2,1)S(1)} %maximum_bitcast_fusion.w_ref, bf16[64,4,384]{2,1,0:T(4,128)(2,1)S(1)} %reshape.299.mix_ref), custom_call_target="tpu_custom_call" | custom-call | tf_op jit(solution)/shard_map/gather_weights/pallas_call | solution.py:166
  33.5 0.2 fusion.21
  34.1 0.3 reshape.302
  34.4 0.2 copy.41
  34.7 0.9 multiply_convert_fusion.2
  35.6 0.8 slice.9
  36.6 1.3 %convolution_bitcast_fusion = f32[256,4,4,96]{0,3,1,2:T(8,128)S(1)} fusion(bf16[4,4,96,96]{3,2,1,0:T(8,128)(2,1)} %bitcast.153, bf16[256,4,96,1]{0,2,3,1:T(8,128)(2,1)S(1)} %bitcast.147), kind=kOutput, calls=%fused_computation.16 | convolution fusion | flops 75497472 | bytes 2064384 | tf_op jit(solution)/shard_map/rjo,jkfo->rkjf/dot_general | solution.py:551
  38.0 0.3 fusion.28
  38.4 2.3 %fusion.3 = (bf16[256,4,384]{0,2,1:T(8,128)(2,1)S(1)}, bf16[256,4,384]{0,2,1:T(8,128)(2,1)S(1)}, bf16[256,4,384]{0,2,1:T(8,128)(2,1)}, f32[4,384,256]{2,1,0:T(8,128)}) fusion(f32[256,4,4,96]{0,3,2,1:T(8,128)S(1)} %copy.48, f32[4,384,256]{2,1,0:T(8,128)S(1)} %fusion.28, bf16[12,384,96]{2,1,0:T(8,128)(2,1)S(1)} %get-tuple-element.23, ...), kind=kOutput, calls=%fused_computation.5 | convolution fusion | flops 81395712 | bytes 8159232 | tf_op jit(solution)/shard_map/rkd,kfd->rkf/dot_general | solution.py:540
  40.8 0.3 fusion.29
  41.1 0.7 copy-done.12
  41.7 1.1 %multiply_reduce_fusion = (f32[4,96]{1,0:T(4,128)S(1)}, f32[256]{0:T(256)S(1)}, f32[4,96,256]{2,1,0:T(8,128)}) fusion(f32[256,4,96]{0,2,1:T(8,128)S(1)} %copy-done.12, f32[4,96]{1,0:T(4,128)S(1)} %mul.198, f32[4,96,256]{2,1,0:T(8,128)S(1)} %fusion.29, bf16[12,384,96]{2,1,0:T(8,128)(2,1)S(1)} %get-tuple-element.23, ...), kind=kOutput, calls=%fused_computation.35 | convolution fusion | flops 76086656 | bytes 2854912 | tf_op jit(solution)/shard_map/rkf,kfd->rkd/dot_general | solution.py:558
  42.9 2.0 %copy.53 = f32[1,256,384]{2,1,0:T(8,128)} copy(f32[1,256,384]{1,2,0:T(8,128)} %bitcast.151) | data formatting | bytes 786432 | tf_op jit(solution)/shard_map/reshape | solution.py:559
  44.8 2.4 %fusion.10 = f32[4,96,256,1]{2,1,3,0:T(8,128)} fusion(bf16[4,4,96,96]{3,2,1,0:T(8,128)(2,1)} %bitcast.154, bf16[256,4,4,96]{0,3,2,1:T(8,128)(2,1)} %bitcast.159), kind=kOutput, calls=%fused_computation.22 | convolution fusion | flops 75497472 | bytes 1474560 | tf_op jit(solution)/shard_map/rkjf,jkfo->rjo/dot_general | solution.py:546
  47.2 2.0 %copy.46 = f32[1,256,384]{2,1,0:T(8,128)} copy(f32[1,256,384]{1,2,0:T(8,128)} %bitcast.158) | data formatting | bytes 786432 | tf_op jit(solution)/shard_map/reshape | solution.py:548
  49.3 0.8 convert_element_type.83
  50.1 1.0 copy.54
  51.1 2.1 %reshape.308 = f32[4,64,384]{2,1,0:T(8,128)} reshape(f32[256,4,96]{2,1,0:T(4,128)} %copy.54) | data formatting | bytes 786432 | tf_op jit(solution)/shard_map/reshape | solution.py:559
  53.3 1.5 %multiply_reduce_fusion.1 = (f32[384]{0:T(512)S(1)}, f32[4,64,384]{2,1,0:T(8,128)S(1)}) fusion(f32[4,384,64]{1,2,0:T(8,128)S(1)} %copy-done.4, f32[4,64]{1,0:T(4,128)S(1)} %div.17, f32[4,64,384]{2,1,0:T(8,128)} %bitcast.156, f32[384]{0:T(512)S(1)} %copy-done.13, f32[4,64,384]{2,1,0:T(8,128)} %reshape.308, f32[384]{0:T(512)S(1)} %copy-done.16, ...), kind=kLoop, calls=%fused_computation.36 | loop fusion | flops 1080960 | bytes 1776128 | tf_op jit(solution)/shard_map/reduce_sum | solution.py:565
  54.7 0.2 convolution_convert_fusion.1
  55.2 1.9 %multiply_convert_fusion.hidden_ref = bf16[4,384,256]{2,1,0:T(8,128)(2,1)S(1)} fusion(f32[4,384,256]{2,1,0:T(8,128)S(1)} %copy-done.8, f32[4,384,256]{2,1,0:T(8,128)} %get-tuple-element.45), kind=kLoop, calls=%fused_computation.15 | loop fusion | flops 2359296 | bytes 3932160 | tf_op jit(solution)/shard_map/convert_element_type | solution.py:544
  57.1 19.2 %exchange_back.1 = (bf16[64,4,384]{2,1,0:T(4,128)(2,1)S(1)}, bf16[8,80,128]{2,1,0:T(8,128)(2,1)S(1)}) custom-call(bf16[64,4,384]{2,1,0:T(4,128)(2,1)S(1)} %bitcast.149, bf16[4,384,256]{2,1,0:T(8,128)(2,1)S(1)} %bitcast.144, bf16[4,384,256]{2,1,0:T(8,128)(2,1)S(1)} %bitcast.145, bf16[4,384,256]{2,1,0:T(8,128)(2,1)S(1)} %multiply_convert_fusion.hidden_ref, ...), custom_call_target="tpu_custom_call" | custom-call | tf_op jit(solution)/shard_map/exchange_back/pallas_call | solution.py:301
  76.3 0.7 copy-done.1
  77.1 2.3 %fusion.18 = (bf16[1,256,384]{2,1,0:T(8,128)(2,1)}, bf16[1,256,384]{2,1,0:T(8,128)(2,1)}, f32[384,256]{0,1:T(8,128)S(1)}) fusion(f32[1,256,384]{2,1,0:T(8,128)} %copy.53, f32[4,384,64]{1,2,0:T(8,128)S(1)} %copy-done.4, bf16[1,256,384]{2,1,0:T(8,128)(2,1)S(1)} %copy-done.6, f32[256]{0:T(256)S(1)} %broadcast_multiply_fusion, f32[384]{0:T(512)S(1)} %copy-done.16, ...), kind=kOutput, calls=%fused_computation.34 | convolution fusion | flops 51806208 | bytes 2693632 | tf_op jit(solution)/shard_map/pb,apc->abc/dot_general | solution.py:584
  79.3 0.3 fusion.23.left_ref
  79.6 0.2 convolution_bitcast_fusion.1.right_ref
  80.0 0.3 copy-done.2
  80.3 28.7 %sum_gradients.1.sums_ref = f32[584,384]{1,0:T(8,128)S(1)} custom-call(bf16[8,80,128]{2,1,0:T(8,128)(2,1)S(1)} %copy-done.2, f32[256,256]{1,0:T(8,128)S(1)} %fusion.23.left_ref, f32[64,64]{1,0:T(8,128)S(1)} %convolution_bitcast_fusion.1.right_ref, f32[384]{0:T(512)S(1)} %fusion.12.in_ref, f32[384]{0:T(512)S(1)} %get-tuple-element.36.outg_ref, ...), custom_call_target="tpu_custom_call" | custom-call | tf_op jit(solution)/shard_map/sum_gradients/pallas_call | solution.py:446
  109.0 0.9 split_sums.1
  (45 shorter events, 1.3 us)
Async XLA Ops:
  0.6 1.8 %copy-start = (bf16[256,256]{1,0:T(8,128)(2,1)S(1)}, bf16[256,256]{1,0:T(8,128)(2,1)}, u32[]{:S(2)}) copy-start(bf16[256,256]{1,0:T(8,128)(2,1)} %param.14) | copy-start | bytes 393220
  0.7 33.1 %copy-start.5 = (bf16[1,256,384]{2,1,0:T(8,128)(2,1)S(1)}, bf16[1,256,384]{2,1,0:T(8,128)(2,1)}, u32[]{:S(2)}) copy-start(bf16[1,256,384]{2,1,0:T(8,128)(2,1)} %param.10) | copy-start | bytes 589828
  0.7 32.9 %copy-start.14 = (bf16[64,64]{1,0:T(8,128)(2,1)S(1)}, bf16[64,64]{1,0:T(8,128)(2,1)}, u32[]{:S(2)}) copy-start(bf16[64,64]{1,0:T(8,128)(2,1)} %param.15) | copy-start | bytes 24580
  0.7 33.1 %copy-start.13 = (f32[384]{0:T(512)S(1)}, f32[384]{0:T(512)}, u32[]{:S(2)}) copy-start(f32[384]{0:T(512)} %param.13) | copy-start | bytes 4612
  33.8 0.9 copy-start.3
  34.4 2.0 %copy-start.10 = (bf16[1,256,384]{2,1,0:T(8,128)(2,1)S(1)}, bf16[1,256,384]{2,1,0:T(8,128)(2,1)}, u32[]{:S(2)}) copy-start(bf16[1,256,384]{2,1,0:T(8,128)(2,1)} %param.11) | copy-start | bytes 589828
  38.4 2.3 %copy-start.7 = (f32[4,384,256]{2,1,0:T(8,128)}, f32[4,384,256]{2,1,0:T(8,128)S(1)}, u32[]{:S(2)}) copy-start(f32[4,384,256]{2,1,0:T(8,128)S(1)} %fusion.28) | copy-start | bytes 4718596
  40.8 1.0 copy-start.12
  42.9 6.4 %copy-start.6 = (bf16[1,256,384]{2,1,0:T(8,128)(2,1)S(1)}, bf16[1,256,384]{2,1,0:T(8,128)(2,1)}, u32[]{:S(2)}) copy-start(bf16[1,256,384]{2,1,0:T(8,128)(2,1)} %param.10) | copy-start | bytes 589828
  44.8 5.3 %copy-start.9 = (f32[4,96,256]{2,1,0:T(8,128)S(1)}, f32[4,96,256]{2,1,0:T(8,128)}, u32[]{:S(2)}) copy-start(f32[4,96,256]{2,1,0:T(8,128)} %get-tuple-element.46) | copy-start | bytes 1179652
  47.2 6.0 %copy-start.4 = (f32[4,384,64]{1,2,0:T(8,128)S(1)}, f32[4,384,64]{1,2,0:T(8,128)}, u32[]{:S(2)}) copy-start(f32[4,384,64]{1,2,0:T(8,128)} %copy-done.3) | copy-start | bytes 1179652
  47.2 6.0 %copy-start.11 = (bf16[1,256,384]{2,1,0:T(8,128)(2,1)S(1)}, bf16[1,256,384]{2,1,0:T(8,128)(2,1)}, u32[]{:S(2)}) copy-start(bf16[1,256,384]{2,1,0:T(8,128)(2,1)} %param.11) | copy-start | bytes 589828
  47.2 6.0 %copy-start.16 = (f32[384]{0:T(512)S(1)}, f32[384]{0:T(512)}, u32[]{:S(2)}) copy-start(f32[384]{0:T(512)} %param.16) | copy-start | bytes 4612
  53.2 1.9 %copy-start.8 = (f32[4,384,256]{2,1,0:T(8,128)S(1)}, f32[4,384,256]{2,1,0:T(8,128)}, u32[]{:S(2)}) copy-start(f32[4,384,256]{2,1,0:T(8,128)} %copy-done.7) | copy-start | bytes 4718596
  57.1 20.0 %copy-start.15 = (f32[384]{0:T(512)S(1)}, f32[384]{0:T(512)}, u32[]{:S(2)}) copy-start(f32[384]{0:T(512)} %param.12) | copy-start | bytes 4612
  76.3 0.7 copy-start.1
  79.3 0.9 copy-start.2

commit v6 on v5

--- a/solution.py
+++ b/solution.py
@@ -136,14 +136,20 @@
         copy.start()
         sends.append(copy)
     local.wait()
-    for copy in sends:
+    swaps = []
+    for first, h in ((0, yh), (3, 1 - yh)):
+        for copy in sends[first : first + 3]:
+            copy.wait_recv()
+        for k in range(4):
+            n = 4 * (first // 3) + k
+            shard = part(2 * k + h)
+            copy = remote(shard, shard, 8 + n, 7 + n, pair)
+            copy.start()
+            swaps.append(copy)
+    exchange.wait()
+    for copy in swaps:
         copy.wait_recv()
-    whole = out_ref.at[pl.ds(half * c, half)]
-    copy = remote(whole, whole, 8, 7, pair)
-    copy.start()
-    exchange.wait()
-    copy.wait_recv()
-    for copy in sends + [copy]:
+    for copy in sends + swaps:
         copy.wait_send()
 
     @pl.when(end)
@@ -173,8 +179,8 @@
         out_specs=(vmem,) * 2,
         scratch_shapes=[
             pltpu.SemaphoreType.DMA,
-            pltpu.SemaphoreType.DMA((9,)),
-            pltpu.SemaphoreType.DMA((8,)),
+            pltpu.SemaphoreType.DMA((16,)),
+            pltpu.SemaphoreType.DMA((15,)),
         ]
         + line_semaphores(mix.shape[0]),
         compiler_params=pltpu.CompilerParams(

time: 110 us -> 110 us (level)
  no operation moved by 1% of the time
where the time goes in v6:
time: 110 us
  Pallas kernels  78.4 us (71%)
  matrix products  12.2 us (11%)
  local copies, waits for them, and re-layouts  11.9 us (11%)
  other arithmetic  6.18 us (6%)
    pallas_call x1, Pallas kernels, gather_weights(): pl.pallas_call(gather_kernel, out_shape=(jax.ShapeDtypeStruct((n, 8 * wid...  29.6 us
    pallas_call x1, Pallas kernels, sum_gradients(): pl.pallas_call(functools.partial(sum_kernel, factor), out_shape=jax.Shape...  28.7 us
    pallas_call x1, Pallas kernels, exchange_back(): pl.pallas_call(back_kernel, out_shape=(jax.ShapeDtypeStruct(mix.shape, mi...  19.2 us
    reshape x2, local copies, waits for them, and re-layouts, shards(): dhid_in = (dhid_in + jnp.einsum('rkf,kfd->rkd', dupper, up_full, preferre...  4.03 us
    dot_general x1, matrix products, shards(): jnp.einsum('rkjf,jkfo->rjo', hidden_grid, down_grid, preferred_element_ty...  2.38 us
    dot_general x1, matrix products, shards(): jnp.einsum('rkd,kfd->rkf', hidden_in, gate_full, preferred_element_type=j...  2.34 us
    dot_general x1, matrix products, shards(): jnp.einsum('pb,apc->abc', left_factor, received, preferred_element_type=j...  2.29 us

profile of v6, /device:TPU:1, one launch (start us, length us, event | category | flops | bytes accessed | tf_op | source)
XLA Modules:
  0.0 109.5 jit_solution(12657387965470118558)
XLA Ops:
  0.7 0.8 mul.198
  1.5 0.9 maximum_bitcast_fusion.w_ref
  2.4 1.2 %fusion.9 = bf16[1,256,384]{2,1,0:T(8,128)(2,1)S(1)} fusion(bf16[256,256]{1,0:T(8,128)(2,1)S(1)} %copy-done, bf16[1,256,384]{2,1,0:T(8,128)(2,1)} %param.10, f32[384]{0:T(512)} %param.12), kind=kOutput, calls=%fused_computation.20 | convolution fusion | flops 50724864 | bytes 525824 | tf_op jit(solution)/shard_map/pb,abc->apc/dot_general | solution.py:531
  3.6 29.6 %gather_weights.1 = (bf16[12,384,96]{2,1,0:T(8,128)(2,1)S(1)}, bf16[64,4,384]{2,1,0:T(4,128)(2,1)S(1)}) custom-call(bf16[12,48,96]{2,1,0:T(8,128)(2,1)S(1)} %maximum_bitcast_fusion.w_ref, bf16[64,4,384]{2,1,0:T(4,128)(2,1)S(1)} %reshape.299.mix_ref), custom_call_target="tpu_custom_call" | custom-call | tf_op jit(solution)/shard_map/gather_weights/pallas_call | solution.py:172
  33.3 0.2 fusion.21
  33.8 0.3 reshape.302
  34.1 0.2 copy.41
  34.4 0.9 multiply_convert_fusion.2
  35.4 0.8 slice.9
  36.3 1.3 %convolution_bitcast_fusion = f32[256,4,4,96]{0,3,1,2:T(8,128)S(1)} fusion(bf16[4,4,96,96]{3,2,1,0:T(8,128)(2,1)} %bitcast.153, bf16[256,4,96,1]{0,2,3,1:T(8,128)(2,1)S(1)} %bitcast.147), kind=kOutput, calls=%fused_computation.16 | convolution fusion | flops 75497472 | bytes 2064384 | tf_op jit(solution)/shard_map/rjo,jkfo->rkjf/dot_general | solution.py:557
  37.8 0.3 fusion.28
  38.1 2.3 %fusion.3 = (bf16[256,4,384]{0,2,1:T(8,128)(2,1)S(1)}, bf16[256,4,384]{0,2,1:T(8,128)(2,1)S(1)}, bf16[256,4,384]{0,2,1:T(8,128)(2,1)}, f32[4,384,256]{2,1,0:T(8,128)}) fusion(f32[256,4,4,96]{0,3,2,1:T(8,128)S(1)} %copy.48, f32[4,384,256]{2,1,0:T(8,128)S(1)} %fusion.28, bf16[12,384,96]{2,1,0:T(8,128)(2,1)S(1)} %get-tuple-element.23, ...), kind=kOutput, calls=%fused_computation.5 | convolution fusion | flops 81395712 | bytes 8159232 | tf_op jit(solution)/shard_map/rkd,kfd->rkf/dot_general | solution.py:546
  40.5 0.3 fusion.29
  40.8 0.7 copy-done.12
  41.5 1.1 %multiply_reduce_fusion = (f32[4,96]{1,0:T(4,128)S(1)}, f32[256]{0:T(256)S(1)}, f32[4,96,256]{2,1,0:T(8,128)}) fusion(f32[256,4,96]{0,2,1:T(8,128)S(1)} %copy-done.12, f32[4,96]{1,0:T(4,128)S(1)} %mul.198, f32[4,96,256]{2,1,0:T(8,128)S(1)} %fusion.29, bf16[12,384,96]{2,1,0:T(8,128)(2,1)S(1)} %get-tuple-element.23, ...), kind=kOutput, calls=%fused_computation.35 | convolution fusion | flops 76086656 | bytes 2854912 | tf_op jit(solution)/shard_map/rkf,kfd->rkd/dot_general | solution.py:564
  42.6 2.0 %copy.53 = f32[1,256,384]{2,1,0:T(8,128)} copy(f32[1,256,384]{1,2,0:T(8,128)} %bitcast.151) | data formatting | bytes 786432 | tf_op jit(solution)/shard_map/reshape | solution.py:565
  44.5 2.4 %fusion.10 = f32[4,96,256,1]{2,1,3,0:T(8,128)} fusion(bf16[4,4,96,96]{3,2,1,0:T(8,128)(2,1)} %bitcast.154, bf16[256,4,4,96]{0,3,2,1:T(8,128)(2,1)} %bitcast.159), kind=kOutput, calls=%fused_computation.22 | convolution fusion | flops 75497472 | bytes 1474560 | tf_op jit(solution)/shard_map/rkjf,jkfo->rjo/dot_general | solution.py:552
  46.9 2.0 %copy.46 = f32[1,256,384]{2,1,0:T(8,128)} copy(f32[1,256,384]{1,2,0:T(8,128)} %bitcast.158) | data formatting | bytes 786432 | tf_op jit(solution)/shard_map/reshape | solution.py:554
  49.0 0.8 convert_element_type.83
  49.8 1.0 copy.54
  50.8 2.1 %reshape.308 = f32[4,64,384]{2,1,0:T(8,128)} reshape(f32[256,4,96]{2,1,0:T(4,128)} %copy.54) | data formatting | bytes 786432 | tf_op jit(solution)/shard_map/reshape | solution.py:565
  53.0 1.5 %multiply_reduce_fusion.1 = (f32[384]{0:T(512)S(1)}, f32[4,64,384]{2,1,0:T(8,128)S(1)}) fusion(f32[4,384,64]{1,2,0:T(8,128)S(1)} %copy-done.4, f32[4,64]{1,0:T(4,128)S(1)} %div.17, f32[4,64,384]{2,1,0:T(8,128)} %bitcast.156, f32[384]{0:T(512)S(1)} %copy-done.13, f32[4,64,384]{2,1,0:T(8,128)} %reshape.308, f32[384]{0:T(512)S(1)} %copy-done.16, ...), kind=kLoop, calls=%fused_computation.36 | loop fusion | flops 1080960 | bytes 1776128 | tf_op jit(solution)/shard_map/reduce_sum | solution.py:571
  54.4 0.2 convolution_convert_fusion.1
  54.9 1.9 %multiply_convert_fusion.hidden_ref = bf16[4,384,256]{2,1,0:T(8,128)(2,1)S(1)} fusion(f32[4,384,256]{2,1,0:T(8,128)S(1)} %copy-done.8, f32[4,384,256]{2,1,0:T(8,128)} %get-tuple-element.45), kind=kLoop, calls=%fused_computation.15 | loop fusion | flops 2359296 | bytes 3932160 | tf_op jit(solution)/shard_map/convert_element_type | solution.py:550
  56.8 19.2 %exchange_back.1 = (bf16[64,4,384]{2,1,0:T(4,128)(2,1)S(1)}, bf16[8,80,128]{2,1,0:T(8,128)(2,1)S(1)}) custom-call(bf16[64,4,384]{2,1,0:T(4,128)(2,1)S(1)} %bitcast.149, bf16[4,384,256]{2,1,0:T(8,128)(2,1)S(1)} %bitcast.144, bf16[4,384,256]{2,1,0:T(8,128)(2,1)S(1)} %bitcast.145, bf16[4,384,256]{2,1,0:T(8,128)(2,1)S(1)} %multiply_convert_fusion.hidden_ref, ...), custom_call_target="tpu_custom_call" | custom-call | tf_op jit(solution)/shard_map/exchange_back/pallas_call | solution.py:307
  76.0 0.7 copy-done.1
  76.8 2.3 %fusion.18 = (bf16[1,256,384]{2,1,0:T(8,128)(2,1)}, bf16[1,256,384]{2,1,0:T(8,128)(2,1)}, f32[384,256]{0,1:T(8,128)S(1)}) fusion(f32[1,256,384]{2,1,0:T(8,128)} %copy.53, f32[4,384,64]{1,2,0:T(8,128)S(1)} %copy-done.4, bf16[1,256,384]{2,1,0:T(8,128)(2,1)S(1)} %copy-done.6, f32[256]{0:T(256)S(1)} %broadcast_multiply_fusion, f32[384]{0:T(512)S(1)} %copy-done.16, ...), kind=kOutput, calls=%fused_computation.34 | convolution fusion | flops 51806208 | bytes 2693632 | tf_op jit(solution)/shard_map/pb,apc->abc/dot_general | solution.py:590
  79.0 0.3 fusion.23.left_ref
  79.3 0.2 convolution_bitcast_fusion.1.right_ref
  79.7 0.3 copy-done.2
  80.0 28.7 %sum_gradients.1.sums_ref = f32[584,384]{1,0:T(8,128)S(1)} custom-call(bf16[8,80,128]{2,1,0:T(8,128)(2,1)S(1)} %copy-done.2, f32[256,256]{1,0:T(8,128)S(1)} %fusion.23.left_ref, f32[64,64]{1,0:T(8,128)S(1)} %convolution_bitcast_fusion.1.right_ref, f32[384]{0:T(512)S(1)} %fusion.12.in_ref, f32[384]{0:T(512)S(1)} %get-tuple-element.36.outg_ref, ...), custom_call_target="tpu_custom_call" | custom-call | tf_op jit(solution)/shard_map/sum_gradients/pallas_call | solution.py:452
  108.7 0.9 split_sums.1
  (45 shorter events, 1.3 us)
Async XLA Ops:
  0.6 1.8 %copy-start = (bf16[256,256]{1,0:T(8,128)(2,1)S(1)}, bf16[256,256]{1,0:T(8,128)(2,1)}, u32[]{:S(2)}) copy-start(bf16[256,256]{1,0:T(8,128)(2,1)} %param.14) | copy-start | bytes 393220
  0.7 32.8 %copy-start.5 = (bf16[1,256,384]{2,1,0:T(8,128)(2,1)S(1)}, bf16[1,256,384]{2,1,0:T(8,128)(2,1)}, u32[]{:S(2)}) copy-start(bf16[1,256,384]{2,1,0:T(8,128)(2,1)} %param.10) | copy-start | bytes 589828
  0.7 32.6 %copy-start.14 = (bf16[64,64]{1,0:T(8,128)(2,1)S(1)}, bf16[64,64]{1,0:T(8,128)(2,1)}, u32[]{:S(2)}) copy-start(bf16[64,64]{1,0:T(8,128)(2,1)} %param.15) | copy-start | bytes 24580
  0.7 32.8 %copy-start.13 = (f32[384]{0:T(512)S(1)}, f32[384]{0:T(512)}, u32[]{:S(2)}) copy-start(f32[384]{0:T(512)} %param.13) | copy-start | bytes 4612
  33.5 0.9 copy-start.3
  34.1 2.0 %copy-start.10 = (bf16[1,256,384]{2,1,0:T(8,128)(2,1)S(1)}, bf16[1,256,384]{2,1,0:T(8,128)(2,1)}, u32[]{:S(2)}) copy-start(bf16[1,256,384]{2,1,0:T(8,128)(2,1)} %param.11) | copy-start | bytes 589828
  38.1 2.3 %copy-start.7 = (f32[4,384,256]{2,1,0:T(8,128)}, f32[4,384,256]{2,1,0:T(8,128)S(1)}, u32[]{:S(2)}) copy-start(f32[4,384,256]{2,1,0:T(8,128)S(1)} %fusion.28) | copy-start | bytes 4718596
  40.5 1.0 copy-start.12
  42.6 6.4 %copy-start.6 = (bf16[1,256,384]{2,1,0:T(8,128)(2,1)S(1)}, bf16[1,256,384]{2,1,0:T(8,128)(2,1)}, u32[]{:S(2)}) copy-start(bf16[1,256,384]{2,1,0:T(8,128)(2,1)} %param.10) | copy-start | bytes 589828
  44.5 5.3 %copy-start.9 = (f32[4,96,256]{2,1,0:T(8,128)S(1)}, f32[4,96,256]{2,1,0:T(8,128)}, u32[]{:S(2)}) copy-start(f32[4,96,256]{2,1,0:T(8,128)} %get-tuple-element.46) | copy-start | bytes 1179652
  46.9 6.0 %copy-start.4 = (f32[4,384,64]{1,2,0:T(8,128)S(1)}, f32[4,384,64]{1,2,0:T(8,128)}, u32[]{:S(2)}) copy-start(f32[4,384,64]{1,2,0:T(8,128)} %copy-done.3) | copy-start | bytes 1179652
  46.9 6.0 %copy-start.11 = (bf16[1,256,384]{2,1,0:T(8,128)(2,1)S(1)}, bf16[1,256,384]{2,1,0:T(8,128)(2,1)}, u32[]{:S(2)}) copy-start(bf16[1,256,384]{2,1,0:T(8,128)(2,1)} %param.11) | copy-start | bytes 589828
  46.9 6.0 %copy-start.16 = (f32[384]{0:T(512)S(1)}, f32[384]{0:T(512)}, u32[]{:S(2)}) copy-start(f32[384]{0:T(512)} %param.16) | copy-start | bytes 4612
  53.0 1.9 %copy-start.8 = (f32[4,384,256]{2,1,0:T(8,128)S(1)}, f32[4,384,256]{2,1,0:T(8,128)}, u32[]{:S(2)}) copy-start(f32[4,384,256]{2,1,0:T(8,128)} %copy-done.7) | copy-start | bytes 4718596
  56.8 20.0 %copy-start.15 = (f32[384]{0:T(512)S(1)}, f32[384]{0:T(512)}, u32[]{:S(2)}) copy-start(f32[384]{0:T(512)} %param.12) | copy-start | bytes 4612
  76.0 0.7 copy-start.1
  79.0 0.9 copy-start.2
